TPU v7x, 256 devices: a whole 4x4x8 slice. The times are simulated.
256 devices in a mesh: half: 2 (over core), cls: 2 (over y_lo), img: 64 (over y_hi, z, x).
Axes of the slice: x: 4, y: 4 (y_hi: 2, y_lo: 2; y = y_hi * 2 + y_lo), z: 8, core: 2. Of those that a mesh axis runs over, the one named last changes fastest.
Arguments:
- images: bfloat16 [2, 32768, 2, 8320], P('half', ('cls', 'img')), may hold values from -8 to 8
- projections: bfloat16 [2, 8, 8, 2, 8320], P('half', 'cls', None, None, 'img'), may hold values from -8 to 8
- ctf_table: float32 [2, 32, 8320], P('half'), may hold values from -1 to 1
- ctf_group: int32 [2, 32768], P('half', ('cls', 'img')), may hold values from 0 to 31
- orient_ids: int32 [2, 32768, 4], P('half', ('cls', 'img')), may hold values from 0 to 7
- trans_ids: int32 [2, 8], P('half'), may hold values from 0 to 24
- inv_sigma: float32 [2, 8320], P('half'), may hold values from 0.5 to 2
- counts: int32 [2, 128], P('half', ('cls', 'img')), may hold values from 1 to 256, 20480 in all within a row
Outputs:
- posterior: bfloat16 [2, 32768, 512], P('half', ('cls', 'img'))
- slab: float32 [2, 8, 8, 2, 8320], P('half', 'cls', None, None, 'img')
- fsc_map: float32 [2, 8, 8, 8320], P('half', 'cls', None, 'img')
Inputs may be any that keep to these rules, and one draw needn't show every extreme that they name: counts[h, s] is the number of live particles of shard s, held in its first slots; each half-set's counts sum to 20480, and the largest is 256.
All inputs are finite; a program needn't handle non-finite values.
Results may differ from a plain program's by a relative error of at most 0.013.
The roundings to bfloat16 on the way count: a program that leaves them out, or rounds other values in their place, can miss the bound.
Values may be sent and summed in bfloat16 or wider, within the bound.
No kernel may reach another device: no remote copies, remote signals or barrier semaphores. Data moves between devices by JAX's collectives and lax.ppermute only.
A program may use at most 192 MiB of HBM per device.

v0:
```python
import math

import jax
import jax.numpy as jnp
from jax import lax
from jax.experimental import pallas as pl
from jax.experimental.pallas import tpu as pltpu
from jax.sharding import PartitionSpec as P


K = 8
BOX = 128
O = 8
TR = 8
TGRID = 5
FC = 8320
G = 32
NP = 256
LANE = 128
TILES = FC // LANE
CHUNK = 640
STEPS = FC // CHUNK
PARTS = (3, 3, 3, 4)
ROWS = 264
NX, NY, NZ = 4, 4, 8
GRAY = (0, 1, 3, 2)
Z_ORDER = (0, -1, 1, 2, -3, -2, -4, -5)
PAIR = ("cls", "img")
VMEM_LIMIT = 56 * 1024 * 1024


def place(index):
    cls, img = divmod(index, 64)
    y_hi, rest = divmod(img, 32)
    z, x = divmod(rest, 4)
    return x, 2 * y_hi + cls, z


def flat(x, y, z):
    x, y, z = x % NX, y % NY, z % NZ
    return (y % 2) * 64 + (y // 2) * 32 + z * 4 + x


def trade(value, mx=0, my=0):
    pairs = []
    for index in range(NX * NY * NZ):
        x, y, z = place(index)
        pairs.append((index, flat(x ^ mx, y ^ my, z)))
    return lax.ppermute(value, PAIR, pairs)


def trade_z(value, odd):
    pairs = []
    for index in range(NX * NY * NZ):
        x, y, z = place(index)
        pairs.append((index, flat(x, y, z + odd if z % 2 else z - odd)))
    return lax.ppermute(value, PAIR, pairs)


def sources(pos_ref, near, far, color):
    dx, dy = (near, far) if color == 0 else (far, near)
    x = pos_ref[0] ^ (dx ^ (dx >> 1))
    y = pos_ref[1] ^ (dy ^ (dy >> 1))
    sign = 2 * (pos_ref[2] % 2) - 1
    start = (y // 2) * 32 + x
    return y % 2, [start + ((pos_ref[2] + sign * dz) & 7) * 4 for dz in Z_ORDER]


def phases(trans_list, count):
    half_width = BOX // 2 + 1
    freq_index = jnp.arange(count, dtype=jnp.int32)
    row_index = freq_index // half_width
    col_index = freq_index % half_width
    wave_x = (row_index - BOX * (row_index >= BOX // 2).astype(jnp.int32)).astype(jnp.float32)
    wave_y = col_index.astype(jnp.float32)
    shift_x = (trans_list % TGRID - TGRID // 2).astype(jnp.float32)
    shift_y = (trans_list // TGRID - TGRID // 2).astype(jnp.float32)
    angle = (
        2.0
        * math.pi
        / BOX
        * (shift_x[:, None] * wave_x[None, :] + shift_y[:, None] * wave_y[None, :])
    )
    return (jnp.cos(angle), jnp.sin(angle))


def iota(shape, dim):
    return lax.broadcasted_iota(jnp.int32, shape, dim)


def split3(value, axis=0):
    high = value.astype(jnp.bfloat16)
    rest = value - high.astype(jnp.float32)
    mid = rest.astype(jnp.bfloat16)
    low = (rest - mid.astype(jnp.float32)).astype(jnp.bfloat16)
    return jnp.concatenate([high, mid, low], axis=axis)


def mm(left, right, dims=((1,), (0,)), precision=None):
    return lax.dot_general(
        left, right, (dims, ((), ())), precision=precision, preferred_element_type=jnp.float32
    )


def pack_kernel(p_ref, out_ref):
    lane = iota((8, LANE), 1)
    sub = iota((8, LANE), 0)
    tails = []
    for color in range(2):
        extra = jnp.zeros((8, LANE), jnp.float32)
        for kl in range(2):
            for c in range(2):
                rows = p_ref[0, color * 2 + kl, :, c, :].astype(jnp.float32)
                group = kl * 2 + c
                start = color * 32 + group * 8
                out_ref[start : start + 8, :] = rows[:, :LANE].astype(jnp.bfloat16)
                first = 2 * (group * 8 + sub)
                extra += jnp.where(lane == first, rows[:, LANE : LANE + 1], 0.0)
                extra += jnp.where(lane == first + 1, rows[:, LANE + 1 : LANE + 2], 0.0)
        tails.append(jnp.sum(extra, axis=0, keepdims=True))
    both = jnp.where(sub == 0, tails[0], tails[1])
    out_ref[64:72, :] = both.astype(jnp.bfloat16)


def pack_sections(projections):
    shape = jax.ShapeDtypeStruct((72, LANE), jnp.bfloat16)
    return pl.pallas_call(pack_kernel, out_shape=shape, name="pack_sections")(projections)


def onehot_rows(group_row):
    onehot = (iota((G, NP), 0) == group_row).astype(jnp.float32)
    return jnp.concatenate([onehot, onehot, onehot], axis=0)


def weight_kernel(image_ref, table_ref, group_ref, out_ref, ctf_ref, onehot_ref):
    @pl.when(pl.program_id(0) == 0)
    def _():
        onehot_ref[...] = onehot_rows(group_ref[...]).T.astype(jnp.bfloat16)

    ctf_ref[...] = mm(onehot_ref[...], split3(table_ref[0]))

    def body(i, carry):
        rows = pl.ds(pl.multiple_of(i * 16, 16), 16)
        for c in range(2):
            value = image_ref[0, rows, c, :].astype(jnp.float32)
            value = (ctf_ref[rows, :] * value).astype(jnp.bfloat16)
            for tile in range(CHUNK // LANE):
                start = (2 * tile + c) * LANE
                out_ref[rows, start : start + LANE] = value[:, tile * LANE : (tile + 1) * LANE]
        return carry

    lax.fori_loop(0, NP // 16, body, 0)


def weight_images(part, images, table, group_row):
    first, count = sum(PARTS[:part]), PARTS[part]
    return pl.pallas_call(
        weight_kernel,
        grid=(count,),
        in_specs=[
            pl.BlockSpec((1, NP, 2, CHUNK), lambda j: (0, 0, 0, first + j)),
            pl.BlockSpec((1, G, CHUNK), lambda j: (0, 0, first + j)),
            pl.BlockSpec((1, NP), lambda j: (0, 0)),
        ],
        out_specs=pl.BlockSpec((NP, 2 * CHUNK), lambda j: (0, j)),
        out_shape=jax.ShapeDtypeStruct((NP, 2 * CHUNK * count), jnp.bfloat16),
        scratch_shapes=[
            pltpu.VMEM((NP, CHUNK), jnp.float32),
            pltpu.VMEM((NP, 3 * G), jnp.bfloat16),
        ],
        compiler_params=pltpu.CompilerParams(vmem_limit_bytes=VMEM_LIMIT),
    )(images, table, group_row)


def start_copies(w_hbms, w_ref, sem_ref):
    step = 0
    for part, count in enumerate(PARTS):
        for n in range(count):
            lanes = slice(n * 2 * CHUNK, (n + 1) * 2 * CHUNK)
            pltpu.make_async_copy(w_hbms[part].at[:, lanes], w_ref.at[step], sem_ref.at[step]).start()
            step += 1


def wait_copy(w_hbms, w_ref, sem_ref, step):
    source = w_hbms[0].at[:, 0 : 2 * CHUNK]
    pltpu.make_async_copy(source, w_ref.at[step], sem_ref.at[step]).wait()


def unpack_sections(pos_ref, a_refs, b_refs, nat_ref, ex_ref):
    lane = iota((32, LANE), 1)
    for color, refs in ((0, a_refs), (1, b_refs)):
        for near in range(4):
            ref = refs[near]

            def body(far, carry, ref=ref, near=near, color=color):
                cls, chunks = sources(pos_ref, near, far, color)
                rows = pl.ds(pl.multiple_of(cls * 64 + color * 32, 32), 32)
                tails = ref[far, 256:264].astype(jnp.float32)
                for slot, j in enumerate(chunks):
                    piece = ref[far, slot * 32 : slot * 32 + 32].astype(jnp.float32)
                    turned = pltpu.roll(piece, 2 * j, 1)
                    here = pl.ds(pl.multiple_of(j * LANE, LANE), LANE)
                    after = pl.ds(pl.multiple_of((j + 1) * LANE, LANE), LANE)
                    pltpu.store(nat_ref.at[rows, here], turned, mask=lane >= 2 * j)
                    pltpu.store(nat_ref.at[rows, after], turned, mask=lane < 2 * j)
                    ex_ref[pl.ds(cls * 128 + color * 64 + j, 1), :] = tails[slot : slot + 1]
                return carry

            lax.fori_loop(0, 4, body, 0)
    for cls in range(2):
        for color in range(2):
            start = cls * 128 + color * 64
            extra = ex_ref[start : start + 64, :].astype(jnp.bfloat16)
            total = jnp.zeros((32, LANE), jnp.float32)
            for u in range(2):
                pick = (iota((32, LANE), 1) == 2 * iota((32, LANE), 0) + u).astype(jnp.float32)
                column = mm(pick.astype(jnp.bfloat16), extra, ((1,), (1,)))
                spread = (iota((64, LANE), 1) == 2 * iota((64, LANE), 0) + u).astype(jnp.float32)
                total += mm(column.astype(jnp.bfloat16), spread.astype(jnp.bfloat16))
            rows = slice(cls * 64 + color * 32, cls * 64 + color * 32 + 32)
            for t in range(1, TILES):
                here = slice(t * LANE, (t + 1) * LANE)
                pltpu.store(nat_ref.at[rows, here], total, mask=lane // 2 == t - 1)


def score_kernel(
    pos_ref, a0, a1, a2, a3, b0, b1, b2, b3, w0, w1, w2, w3, table_ref, inv_ref,
    cos_ref, sin_ref, group_ref, orient_ref, left_ref, right_ref,
    nat_ref, ex_ref, shift_ref, acc_ref, norm_ref, w_ref, sem_ref,
):
    w_hbms = (w0, w1, w2, w3)
    start_copies(w_hbms, w_ref, sem_ref)
    unpack_sections(pos_ref, (a0, a1, a2, a3), (b0, b1, b2, b3), nat_ref, ex_ref)
    acc_ref[...] = jnp.zeros_like(acc_ref)
    norm_ref[...] = jnp.zeros_like(norm_ref)

    def shift(step, slot):
        for tile in range(CHUNK // LANE):
            here = pl.ds(pl.multiple_of(step * CHUNK + tile * LANE, LANE), LANE)
            inverse = jnp.broadcast_to(inv_ref[0:1, here], (8, LANE))
            cosine = jnp.broadcast_to(cos_ref[:, here][:, None, :], (TR, O, LANE))
            sine = jnp.broadcast_to(sin_ref[:, here][:, None, :], (TR, O, LANE))
            start = 2 * tile * LANE
            for k in range(K):
                real = (nat_ref[k * 16 : k * 16 + 8, here] * inverse)[None]
                imag = (nat_ref[k * 16 + 8 : k * 16 + 16, here] * inverse)[None]
                rows = slice(k * 64, k * 64 + 64)
                shift_ref[slot, rows, start : start + LANE] = (
                    (real * cosine - imag * sine).reshape(TR * O, LANE).astype(jnp.bfloat16)
                )
                shift_ref[slot, rows, start + LANE : start + 2 * LANE] = (
                    (real * sine + imag * cosine).reshape(TR * O, LANE).astype(jnp.bfloat16)
                )
        lanes = pl.ds(pl.multiple_of(step * CHUNK, LANE), CHUNK)
        table = table_ref[0, :, lanes]
        powers = []
        for k in range(K):
            real = nat_ref[k * 16 : k * 16 + 8, lanes]
            imag = nat_ref[k * 16 + 8 : k * 16 + 16, lanes]
            powers.append(real * real + imag * imag)
        power = jnp.concatenate(powers, axis=0)
        ctf_power = table * table * inv_ref[0:1, lanes]
        norm_ref[...] += mm(power, ctf_power, ((1,), (1,)), lax.Precision.HIGHEST)

    def multiply(step, slot):
        acc_ref[...] += mm(shift_ref[slot], w_ref[step], ((1,), (1,)))

    shift(0, 0)

    def body(j, carry):
        wait_copy(w_hbms, w_ref, sem_ref, 2 * j)
        wait_copy(w_hbms, w_ref, sem_ref, 2 * j + 1)
        shift(2 * j + 1, 1)
        multiply(2 * j, 0)
        shift(2 * j + 2, 0)
        multiply(2 * j + 1, 1)
        return carry

    lax.fori_loop(0, STEPS // 2, body, 0)
    wait_copy(w_hbms, w_ref, sem_ref, STEPS - 1)
    multiply(STEPS - 1, 0)

    wide = K * TR * O
    row = iota((wide, K * O), 0)
    widen = (iota((wide, K * O), 1) == (row // (TR * O)) * O + row % O).astype(jnp.float32)
    norm_wide = mm(widen, norm_ref[...], precision=lax.Precision.HIGHEST)
    onehot3 = onehot_rows(group_ref[...]).astype(jnp.bfloat16)
    scores = acc_ref[...] - 0.5 * mm(split3(norm_wide, 1), onehot3)
    orient = iota((wide, NP), 0) % O
    mask = orient_ref[0:1, :] == orient
    for n in range(1, 4):
        mask = mask | (orient_ref[n : n + 1, :] == orient)
    top = jnp.max(jnp.where(mask, scores, -jnp.inf), axis=0, keepdims=True)
    expo = jnp.exp(jnp.where(mask, scores - top, -jnp.inf))
    total = jnp.sum(expo, axis=0, keepdims=True)
    live = (iota((1, NP), 1) < pos_ref[3]).astype(jnp.float32)
    weights = expo / total * live
    rounded = weights.astype(jnp.bfloat16)
    for cls in range(2):
        for color, out in ((0, left_ref), (1, right_ref)):
            k = cls * 4 + color * 2
            out[cls * 128 : cls * 128 + 128, :] = rounded[k * 64 : k * 64 + 128, :]


def order_kernel(left_ref, right_ref, post_ref):
    wide = K * TR * O
    row, col = iota((wide, wide), 0), iota((wide, wide), 1)
    target = (row // (TR * O)) * (TR * O) + (row % O) * TR + (row // O) % TR
    order = (col == target).astype(jnp.float32).astype(jnp.bfloat16)
    rows = []
    for cls in range(2):
        for ref in (left_ref, right_ref):
            rows.append(ref[cls * 128 : cls * 128 + 128, :].astype(jnp.float32))
    turned = jnp.concatenate(rows, axis=0).T.astype(jnp.bfloat16)
    post_ref[0] = mm(turned, order).astype(jnp.bfloat16)


def order_posterior(left, right):
    return pl.pallas_call(
        order_kernel,
        out_shape=jax.ShapeDtypeStruct((1, NP, K * TR * O), jnp.bfloat16),
        name="order_posterior",
    )(left, right)


SMEM = pl.BlockSpec(memory_space=pltpu.SMEM)
VMEM = pl.BlockSpec(memory_space=pltpu.VMEM)
ANY = pl.BlockSpec(memory_space=pl.ANY)


def score(pos, a, b, weighted, table, inverse, cosine, sine, group_row, orient):
    wide = K * O * TR
    return pl.pallas_call(
        score_kernel,
        in_specs=[SMEM] + [VMEM] * 8 + [ANY] * 4 + [VMEM] * 6,
        out_specs=[VMEM] * 2,
        scratch_shapes=[
            pltpu.VMEM((128, FC), jnp.float32),
            pltpu.VMEM((256, LANE), jnp.float32),
            pltpu.VMEM((2, wide, 2 * CHUNK), jnp.bfloat16),
            pltpu.VMEM((wide, NP), jnp.float32),
            pltpu.VMEM((K * O, G), jnp.float32),
            pltpu.VMEM((STEPS, NP, 2 * CHUNK), jnp.bfloat16),
            pltpu.SemaphoreType.DMA((STEPS,)),
        ],
        out_shape=[
            jax.ShapeDtypeStruct((wide // 2, NP), jnp.bfloat16),
            jax.ShapeDtypeStruct((wide // 2, NP), jnp.bfloat16),
        ],
        compiler_params=pltpu.CompilerParams(vmem_limit_bytes=VMEM_LIMIT),
        name="score",
    )(pos, *a, *b, *weighted, table, inverse, cosine, sine, group_row, orient)


def back_kernel(
    color, pos_ref, post_ref, w0, w1, w2, w3, cos_ref, sin_ref, p0, p1, p2, p3,
    slab_ref, sum_ref, ex_ref, w_ref, sem_ref,
):
    w_hbms = (w0, w1, w2, w3)
    start_copies(w_hbms, w_ref, sem_ref)

    def multiply(step, slot):
        sum_ref[slot] = mm(post_ref[...], w_ref[step])

    def combine(step, slot):
        for tile in range(CHUNK // LANE):
            here = pl.ds(pl.multiple_of(step * CHUNK + tile * LANE, LANE), LANE)
            cosine = jnp.broadcast_to(cos_ref[:, here][:, None, :], (TR, O, LANE))
            sine = jnp.broadcast_to(sin_ref[:, here][:, None, :], (TR, O, LANE))
            start = 2 * tile * LANE
            for k in range(4):
                rows = slice(k * 64, k * 64 + 64)
                real = sum_ref[slot, rows, start : start + LANE].reshape(TR, O, LANE)
                imag = sum_ref[slot, rows, start + LANE : start + 2 * LANE].reshape(TR, O, LANE)
                slab_ref[k * 16 : k * 16 + 8, here] = jnp.sum(
                    real * cosine + imag * sine, axis=0
                )
                slab_ref[k * 16 + 8 : k * 16 + 16, here] = jnp.sum(
                    imag * cosine - real * sine, axis=0
                )

    wait_copy(w_hbms, w_ref, sem_ref, 0)
    multiply(0, 0)

    def body(j, carry):
        wait_copy(w_hbms, w_ref, sem_ref, 2 * j + 1)
        wait_copy(w_hbms, w_ref, sem_ref, 2 * j + 2)
        multiply(2 * j + 1, 1)
        combine(2 * j, 0)
        multiply(2 * j + 2, 0)
        combine(2 * j + 1, 1)
        return carry

    lax.fori_loop(0, STEPS // 2, body, 0)
    combine(STEPS - 1, 0)

    lane = iota((32, LANE), 1)
    for cls in range(2):
        rows = slice(cls * 32, cls * 32 + 32)
        tails = jnp.zeros((32, LANE), jnp.float32)
        for t in range(1, TILES):
            tails = jnp.where(lane // 2 == t - 1, slab_ref[rows, t * LANE : (t + 1) * LANE], tails)
        tails = tails.astype(jnp.bfloat16)
        total = jnp.zeros((64, LANE), jnp.float32)
        for u in range(2):
            pick = (iota((64, LANE), 1) == 2 * iota((64, LANE), 0) + u).astype(jnp.float32)
            column = mm(pick.astype(jnp.bfloat16), tails, ((1,), (1,)))
            spread = (iota((32, LANE), 1) == 2 * iota((32, LANE), 0) + u).astype(jnp.float32)
            total += mm(column.astype(jnp.bfloat16), spread.astype(jnp.bfloat16))
        ex_ref[cls * 64 : cls * 64 + 64, :] = total
    for near, out in enumerate((p0, p1, p2, p3)):

        def pack(far, carry, near=near, out=out):
            cls, chunks = sources(pos_ref, near, far, color)
            rows = pl.ds(pl.multiple_of(cls * 32, 32), 32)
            tails = []
            for slot, j in enumerate(chunks):
                here = pl.ds(pl.multiple_of(j * LANE, LANE), LANE)
                after = pl.ds(pl.multiple_of((j + 1) * LANE, LANE), LANE)
                both = jnp.where(lane >= 2 * j, slab_ref[rows, here], slab_ref[rows, after])
                main = pltpu.roll(both, LANE - 2 * j, 1)
                tails.append(ex_ref[pl.ds(cls * 64 + j, 1), :])
                out[far, slot * 32 : slot * 32 + 32, :] = main.astype(jnp.bfloat16)
            out[far, 256:264, :] = jnp.concatenate(tails, axis=0).astype(jnp.bfloat16)
            return carry

        lax.fori_loop(0, 4, pack, 0)


def project_back(color, pos, post, weighted, cosine, sine):
    def kernel(*refs):
        back_kernel(color, *refs)

    return pl.pallas_call(
        kernel,
        in_specs=[SMEM, VMEM] + [ANY] * 4 + [VMEM] * 2,
        out_specs=[VMEM] * 4,
        scratch_shapes=[
            pltpu.VMEM((64, FC), jnp.float32),
            pltpu.VMEM((2, NP, 2 * CHUNK), jnp.float32),
            pltpu.VMEM((128, LANE), jnp.float32),
            pltpu.VMEM((STEPS, NP, 2 * CHUNK), jnp.bfloat16),
            pltpu.SemaphoreType.DMA((STEPS,)),
        ],
        out_shape=[jax.ShapeDtypeStruct((4, ROWS, LANE), jnp.bfloat16)] * 4,
        compiler_params=pltpu.CompilerParams(vmem_limit_bytes=VMEM_LIMIT),
    )(pos, post, *weighted, cosine, sine)


def finish_kernel(own_ref, partner_ref, slab_ref, product_ref):
    lane = iota((8, LANE), 1)
    sub = iota((8, LANE), 0)

    def tails(row, group):
        first = 2 * (group * 8 + sub)
        wide = jnp.broadcast_to(row, (8, LANE))
        one = jnp.sum(jnp.where(lane == first, wide, 0.0), axis=1, keepdims=True)
        two = jnp.sum(jnp.where(lane == first + 1, wide, 0.0), axis=1, keepdims=True)
        return jnp.concatenate([one, two], axis=1)

    for color in range(2):
        base = color * 32
        own_row = own_ref[64 + color : 65 + color, :]
        partner_row = partner_ref[64:72, :].astype(jnp.float32)[color : color + 1]
        for kl in range(2):
            k = color * 2 + kl
            main, edge = 0.0, 0.0
            for c in range(2):
                group = kl * 2 + c
                rows = slice(base + group * 8, base + group * 8 + 8)
                own = own_ref[rows, :]
                own_tail = tails(own_row, group)
                slab_ref[0, k, :, c, 0:LANE] = own
                slab_ref[0, k, :, c, LANE : LANE + 2] = own_tail
                main += own * partner_ref[rows, :].astype(jnp.float32)
                edge += own_tail * tails(partner_row, group)
            product_ref[0, k, :, 0:LANE] = main
            product_ref[0, k, :, LANE : LANE + 2] = edge


def finish(own, partner):
    return pl.pallas_call(
        finish_kernel,
        out_shape=(
            jax.ShapeDtypeStruct((1, 4, O, 2, 130), jnp.float32),
            jax.ShapeDtypeStruct((1, 4, O, 130), jnp.float32),
        ),
        name="finish",
    )(own, partner)


def regroup_kernel(own_ref, got_ref, left_ref, right_ref):
    tails = ([], [])
    for slot in range(NZ):
        ref = own_ref if slot < 4 else got_ref
        last = ref[slot % 4, 64:72, :].astype(jnp.float32)
        for color, out in ((0, left_ref), (1, right_ref)):
            out[0, slot * 32 : slot * 32 + 32, :] = ref[slot % 4, color * 32 : color * 32 + 32, :]
            tails[color].append(last[color : color + 1])
    left_ref[0, 256:264, :] = jnp.concatenate(tails[0], axis=0).astype(jnp.bfloat16)
    right_ref[0, 256:264, :] = jnp.concatenate(tails[1], axis=0).astype(jnp.bfloat16)


def regroup(own, got):
    shape = jax.ShapeDtypeStruct((1, ROWS, LANE), jnp.bfloat16)
    return pl.pallas_call(regroup_kernel, out_shape=(shape, shape), name="regroup")(own, got)


def ungroup_kernel(l0_ref, l1_ref, r0_ref, r1_ref, keep_ref, send_ref):
    sub = iota((8, LANE), 0)
    tails = []
    for first, second in ((l0_ref, l1_ref), (r0_ref, r1_ref)):
        tails.append(first[0, 256:264, :] + second[0, 256:264, :].astype(jnp.float32))
    for slot in range(NZ):
        parts = []
        rows = slice(slot * 32, slot * 32 + 32)
        for first, second in ((l0_ref, l1_ref), (r0_ref, r1_ref)):
            parts.append(first[0, rows, :] + second[0, rows, :].astype(jnp.float32))
        left, right = tails[0][slot : slot + 1], tails[1][slot : slot + 1]
        parts.append(jnp.where(sub == 0, left, jnp.where(sub == 1, right, 0.0)))
        value = jnp.concatenate(parts, axis=0)
        if slot < 4:
            keep_ref[slot] = value
        else:
            send_ref[slot - 4] = value.astype(jnp.bfloat16)


def ungroup(l0, l1, r0, r1):
    return pl.pallas_call(
        ungroup_kernel,
        out_shape=(
            jax.ShapeDtypeStruct((4, 72, LANE), jnp.float32),
            jax.ShapeDtypeStruct((4, 72, LANE), jnp.bfloat16),
        ),
        name="ungroup",
    )(l0, l1, r0, r1)


def added(parts):
    total = parts[0].astype(jnp.float32)
    for part in parts[1:]:
        total = total + part.astype(jnp.float32)
    return total


def run(images, projections, ctf_table, ctf_group, orient_ids, trans_ids, inv_sigma, counts):
    cls, img = lax.axis_index("cls"), lax.axis_index("img")
    pos = jnp.stack(
        [img % 4, 2 * (img // 32) + cls, (img // 4) % 8, counts[0, 0]]
    ).astype(jnp.int32)
    cosine, sine = phases(trans_ids[0], FC)
    weighted = []
    for part in range(len(PARTS)):
        weighted.append(weight_images(part, images, ctf_table, ctf_group))

    along = pack_sections(projections)[None]
    for odd in (-1, 1):
        along = jnp.concatenate([along, trade_z(along, odd)])
    got = trade_z(along, -3)
    left, right = regroup(along, got)
    for mask in (1, 3):
        left = jnp.concatenate([left, trade(left, my=mask)])
        right = jnp.concatenate([right, trade(right, mx=mask)])
    lefts, rights = [left], [right]
    for mask in GRAY[1:]:
        lefts.append(trade(left, mx=mask))
    for mask in GRAY[1:]:
        rights.append(trade(right, my=mask))

    post_left, post_right = score(
        pos, lefts, rights, weighted, ctf_table, inv_sigma, cosine, sine, ctf_group, orient_ids[0].T
    )

    pieces = project_back(0, pos, post_left, weighted, cosine, sine)
    left = added([pieces[0]] + [trade(pieces[d], mx=GRAY[d]) for d in range(1, 4)])
    pieces = project_back(1, pos, post_right, weighted, cosine, sine)
    parts = [pieces[0]]
    for d in range(1, 4):
        parts.append(trade(pieces[d], my=GRAY[d]))
    right = added(parts)
    posterior = order_posterior(post_left, post_right)
    left = added([left[:2], trade(left[2:].astype(jnp.bfloat16), my=3)])
    right = added([right[:2], trade(right[2:].astype(jnp.bfloat16), mx=3)])
    left_got = trade(left[1:].astype(jnp.bfloat16), my=1)
    right_got = trade(right[1:].astype(jnp.bfloat16), mx=1)
    own, sent = ungroup(left[:1], left_got, right[:1], right_got)
    own = own + trade_z(sent, -3).astype(jnp.float32)
    for odd, size in ((1, 2), (-1, 1)):
        own = added([own[:size], trade_z(own[size:].astype(jnp.bfloat16), odd)])
    own = own[0]
    partner = lax.ppermute(own.astype(jnp.bfloat16), "half", [(0, 1), (1, 0)])
    slab, product = finish(own, partner)
    return (posterior, slab, product)


def solution(mesh):
    return jax.shard_map(
        run,
        mesh=mesh,
        in_specs=(
            P("half", ("cls", "img"), None, None),
            P("half", "cls", None, None, "img"),
            P("half", None, None),
            P("half", ("cls", "img")),
            P("half", ("cls", "img"), None),
            P("half", None),
            P("half", None),
            P("half", ("cls", "img")),
        ),
        out_specs=(
            P("half", ("cls", "img"), None),
            P("half", "cls", None, None, "img"),
            P("half", "cls", None, "img"),
        ),
        check_vma=False,
    )
```

profile of v0, /device:TPU:1, one launch (start us, length us, event | category | flops | bytes accessed | tf_op | source)
XLA Modules:
  0.0 163.1 jit_solution(6999430302269697342)
XLA Ops:
  2.2 2.5 %collective-permute-start = (bf16[1,72,128]{2,1,0:T(8,128)(2,1)}, bf16[1,72,128]{2,1,0:T(8,128)(2,1)S(1)}, u32[]{:S(2)}, u32[]{:S(2)}) collective-permute-start(bf16[1,72,128]{2,1,0:T(8,128)(2,1)} %bitcast.27), channel_id=1, source_target_pairs={{0,4},{1,5},{2,6},{3,7},{4,0},{5,1},{6,2},{7,3},{8,12},{9,13},{10,... | collective-permute-start | bytes 55304 | tf_op jit(solution)/shard_map/ppermute | solution.py:57
  6.7 5.4 %collective-permute-start.1 = (bf16[2,72,128]{2,1,0:T(8,128)(2,1)S(1)}, bf16[2,72,128]{2,1,0:T(8,128)(2,1)S(1)}, u32[]{:S(2)}, u32[]{:S(2)}) collective-permute-start(bf16[2,72,128]{2,1,0:T(8,128)(2,1)S(1)} %pad_maximum_fusion.3), channel_id=1, source_target_pairs={{0,28},{1,29},{2,30},{3,31},{4,8},{5,9},{6,10},{7,11},{8,4},{9,5},... | collective-permute-start | bytes 110600 | tf_op jit(solution)/shard_map/ppermute | solution.py:57
  15.9 4.1 %collective-permute-done.2.got_ref = bf16[4,72,128]{2,1,0:T(8,128)(2,1)S(1)} collective-permute-done((bf16[4,72,128]{2,1,0:T(8,128)(2,1)S(1)}, bf16[4,72,128]{2,1,0:T(8,128)(2,1)S(1)}, u32[]{:S(2)}, u32[]{:S(2)}) %collective-permute-start.2) | collective-permute-done | bytes 73760 | tf_op jit(solution)/shard_map/ppermute | solution.py:57
  26.6 2.5 %collective-permute-start.9 = (bf16[2,264,128]{2,1,0:T(8,128)(2,1)S(1)}, bf16[2,264,128]{2,1,0:T(8,128)(2,1)S(1)}, u32[]{:S(2)}, u32[]{:S(2)}) collective-permute-start(bf16[2,264,128]{2,1,0:T(8,128)(2,1)S(1)} %pad_maximum_fusion.1), channel_id=1, source_target_pairs={{0,3},{1,2},{2,1},{3,0},{4,7},{5,6},{6,5},{7,4},{8,11},{9,10},{10,... | collective-permute-start | bytes 405512 | tf_op jit(solution)/shard_map/ppermute | solution.py:49
  30.0 2.8 %collective-permute-start.4 = (bf16[2,264,128]{2,1,0:T(8,128)(2,1)S(1)}, bf16[2,264,128]{2,1,0:T(8,128)(2,1)S(1)}, u32[]{:S(2)}, u32[]{:S(2)}) collective-permute-start(bf16[2,264,128]{2,1,0:T(8,128)(2,1)S(1)} %pad_maximum_fusion), channel_id=1, source_target_pairs={{0,96},{1,97},{2,98},{3,99},{4,100},{5,101},{6,102},{7,103},{8,104... | collective-permute-start | bytes 405512 | tf_op jit(solution)/shard_map/ppermute | solution.py:49
  33.8 2.0 %collective-permute-start.11 = (bf16[4,264,128]{2,1,0:T(8,128)(2,1)S(1)}, bf16[4,264,128]{2,1,0:T(8,128)(2,1)S(1)}, u32[]{:S(2)}, u32[]{:S(2)}) collective-permute-start(bf16[4,264,128]{2,1,0:T(8,128)(2,1)S(1)} %constant_dynamic-update-slice_fusion.3.b0), channel_id=1, source_target_pairs={{0,96},{1,97},{2,98},{3,99},{4,100},{5,101},{6,102},{7,103},{8,104... | collective-permute-start | bytes 811016 | tf_op jit(solution)/shard_map/ppermute | solution.py:49
  37.2 2.2 %collective-permute-start.6 = (bf16[4,264,128]{2,1,0:T(8,128)(2,1)S(1)}, bf16[4,264,128]{2,1,0:T(8,128)(2,1)S(1)}, u32[]{:S(2)}, u32[]{:S(2)}) collective-permute-start(bf16[4,264,128]{2,1,0:T(8,128)(2,1)S(1)} %constant_dynamic-update-slice_fusion.a0), channel_id=1, source_target_pairs={{0,3},{1,2},{2,1},{3,0},{4,7},{5,6},{6,5},{7,4},{8,11},{9,10},{10,... | collective-permute-start | bytes 811016 | tf_op jit(solution)/shard_map/ppermute | solution.py:49
  42.5 6.6 %shard_map.106.w3.refs_5_ = bf16[256,5120]{1,0:T(8,128)(2,1)} custom-call(bf16[1,256,2,8320]{3,2,1,0:T(2,128)(2,1)} %image_ref.7, f32[1,32,8320]{2,1,0:T(8,128)} %table_ref.9, s32[1,256]{1,0:T(1,128)} %group_ref.9), custom_call_target="tpu_custom_call" | custom-call | tf_op jit(solution)/shard_map/pallas_call | solution.py:157
  49.1 5.5 %shard_map.103.w0.refs_2_ = bf16[256,3840]{1,0:T(8,128)(2,1)} custom-call(bf16[1,256,2,8320]{3,2,1,0:T(2,128)(2,1)} %image_ref.7, f32[1,32,8320]{2,1,0:T(8,128)} %table_ref.9, s32[1,256]{1,0:T(1,128)} %group_ref.9), custom_call_target="tpu_custom_call" | custom-call | tf_op jit(solution)/shard_map/pallas_call | solution.py:157
  54.6 5.5 %shard_map.104.w1.refs_3_ = bf16[256,3840]{1,0:T(8,128)(2,1)} custom-call(bf16[1,256,2,8320]{3,2,1,0:T(2,128)(2,1)} %image_ref.7, f32[1,32,8320]{2,1,0:T(8,128)} %table_ref.9, s32[1,256]{1,0:T(1,128)} %group_ref.9), custom_call_target="tpu_custom_call" | custom-call | tf_op jit(solution)/shard_map/pallas_call | solution.py:157
  60.0 5.5 %shard_map.105.w2.refs_4_ = bf16[256,3840]{1,0:T(8,128)(2,1)} custom-call(bf16[1,256,2,8320]{3,2,1,0:T(2,128)(2,1)} %image_ref.7, f32[1,32,8320]{2,1,0:T(8,128)} %table_ref.9, s32[1,256]{1,0:T(1,128)} %group_ref.9), custom_call_target="tpu_custom_call" | custom-call | tf_op jit(solution)/shard_map/pallas_call | solution.py:157
  67.8 17.5 %score.1 = (bf16[256,256]{1,0:T(8,128)(2,1)}, bf16[256,256]{1,0:T(8,128)(2,1)}) custom-call(s32[4]{0:T(128)} %pad_add_fusion.pos_ref.refs_0_, bf16[4,264,128]{2,1,0:T(8,128)(2,1)} %copy-done, bf16[4,264,128]{2,1,0:T(8,128)(2,1)} %copy-done.8, bf16[4,264,128]{2,1,0:T(8,128)(2,1)} %copy-done.9, bf16[4,264,128]{2,1,0:T(8,128)(2,1)} %copy-done.10, ...), custom_call_target="tpu_custom_call" | custom-call | tf_op jit(solution)/shard_map/score/pallas_call | solution.py:333
  85.3 9.4 %shard_map.108 = (bf16[4,264,128]{2,1,0:T(8,128)(2,1)}, bf16[4,264,128]{2,1,0:T(8,128)(2,1)}, bf16[4,264,128]{2,1,0:T(8,128)(2,1)}, bf16[4,264,128]{2,1,0:T(8,128)(2,1)}) custom-call(s32[4]{0:T(128)} %pad_add_fusion.pos_ref.refs_0_, bf16[256,256]{1,0:T(8,128)(2,1)} %get-tuple-element.22.right_ref.refs_1_, bf16[256,3840]{1,0:T(8,128)(2,1)} %shard_map.103.w0.refs_2_, ...), custom_call_target="tpu_custom_call" | custom-call | tf_op jit(solution)/shard_map/pallas_call | solution.py:434
  95.3 1.9 %collective-permute-start.19 = (bf16[4,264,128]{2,1,0:T(8,128)(2,1)}, bf16[4,264,128]{2,1,0:T(8,128)(2,1)S(1)}, u32[]{:S(2)}, u32[]{:S(2)}) collective-permute-start(bf16[4,264,128]{2,1,0:T(8,128)(2,1)} %get-tuple-element.29), channel_id=1, source_target_pairs={{0,96},{1,97},{2,98},{3,99},{4,100},{5,101},{6,102},{7,103},{8,104... | collective-permute-start | bytes 811016 | tf_op jit(solution)/shard_map/ppermute | solution.py:49
  98.0 9.4 %shard_map.107 = (bf16[4,264,128]{2,1,0:T(8,128)(2,1)}, bf16[4,264,128]{2,1,0:T(8,128)(2,1)}, bf16[4,264,128]{2,1,0:T(8,128)(2,1)}, bf16[4,264,128]{2,1,0:T(8,128)(2,1)}) custom-call(s32[4]{0:T(128)} %pad_add_fusion.pos_ref.refs_0_, bf16[256,256]{1,0:T(8,128)(2,1)} %get-tuple-element.21.left_ref.refs_1_, bf16[256,3840]{1,0:T(8,128)(2,1)} %shard_map.103.w0.refs_2_, ...), custom_call_target="tpu_custom_call" | custom-call | tf_op jit(solution)/shard_map/pallas_call | solution.py:434
  113.3 4.3 %collective-permute-done.14 = bf16[4,264,128]{2,1,0:T(8,128)(2,1)S(1)} collective-permute-done((bf16[4,264,128]{2,1,0:T(8,128)(2,1)}, bf16[4,264,128]{2,1,0:T(8,128)(2,1)S(1)}, u32[]{:S(2)}, u32[]{:S(2)}) %collective-permute-start.14) | collective-permute-done | bytes 270368 | tf_op jit(solution)/shard_map/ppermute | solution.py:49
  117.8 2.2 %collective-permute-start.16 = (bf16[2,264,128]{2,1,0:T(8,128)(2,1)S(1)}, bf16[2,264,128]{2,1,0:T(8,128)(2,1)S(1)}, u32[]{:S(2)}, u32[]{:S(2)}) collective-permute-start(bf16[2,264,128]{2,1,0:T(8,128)(2,1)S(1)} %slice.79), channel_id=1, source_target_pairs={{0,96},{1,97},{2,98},{3,99},{4,100},{5,101},{6,102},{7,103},{8,104... | collective-permute-start | bytes 405512 | tf_op jit(solution)/shard_map/ppermute | solution.py:49
  120.1 3.1 %collective-permute-done.16 = bf16[2,264,128]{2,1,0:T(8,128)(2,1)S(1)} collective-permute-done((bf16[2,264,128]{2,1,0:T(8,128)(2,1)S(1)}, bf16[2,264,128]{2,1,0:T(8,128)(2,1)S(1)}, u32[]{:S(2)}, u32[]{:S(2)}) %collective-permute-start.16) | collective-permute-done | bytes 135200 | tf_op jit(solution)/shard_map/ppermute | solution.py:49
  124.7 2.1 %collective-permute-done.17.l1_ref = bf16[1,264,128]{2,1,0:T(8,128)(2,1)S(1)} collective-permute-done((bf16[1,264,128]{2,1,0:T(8,128)(2,1)S(1)}, bf16[1,264,128]{2,1,0:T(8,128)(2,1)S(1)}, u32[]{:S(2)}, u32[]{:S(2)}) %collective-permute-start.17) | collective-permute-done | bytes 67616 | tf_op jit(solution)/shard_map/ppermute | solution.py:49
  130.8 4.4 %collective-permute-done.23 = bf16[4,72,128]{2,1,0:T(8,128)(2,1)S(1)} collective-permute-done((bf16[4,72,128]{2,1,0:T(8,128)(2,1)}, bf16[4,72,128]{2,1,0:T(8,128)(2,1)S(1)}, u32[]{:S(2)}, u32[]{:S(2)}) %collective-permute-start.23) | collective-permute-done | bytes 73760 | tf_op jit(solution)/shard_map/ppermute | solution.py:57
  137.4 2.8 %collective-permute-done.24 = bf16[2,72,128]{2,1,0:T(8,128)(2,1)S(1)} collective-permute-done((bf16[2,72,128]{2,1,0:T(8,128)(2,1)S(1)}, bf16[2,72,128]{2,1,0:T(8,128)(2,1)S(1)}, u32[]{:S(2)}, u32[]{:S(2)}) %collective-permute-start.24) | collective-permute-done | bytes 36896 | tf_op jit(solution)/shard_map/ppermute | solution.py:57
  140.3 2.6 %collective-permute-done.25 = bf16[1,72,128]{2,1,0:T(8,128)(2,1)S(1)} collective-permute-done((bf16[1,72,128]{2,1,0:T(8,128)(2,1)S(1)}, bf16[1,72,128]{2,1,0:T(8,128)(2,1)S(1)}, u32[]{:S(2)}, u32[]{:S(2)}) %collective-permute-start.25) | collective-permute-done | bytes 18464 | tf_op jit(solution)/shard_map/ppermute | solution.py:57
  143.6 15.4 %collective-permute-start.26 = (bf16[72,128]{1,0:T(8,128)(2,1)S(1)}, bf16[72,128]{1,0:T(8,128)(2,1)S(1)}, u32[]{:S(2)}, u32[]{:S(2)}) collective-permute-start(bf16[72,128]{1,0:T(8,128)(2,1)S(1)} %get-tuple-element.35), channel_id=1, source_target_pairs={{0,128},{128,0},{1,129},{129,1},{2,130},{130,2},{3,131},{131,3},{4... | collective-permute-start | bytes 55304 | tf_op jit(solution)/shard_map/ppermute | solution.py:591
  158.9 2.1 %order_posterior.1 = bf16[1,256,512]{2,1,0:T(8,128)(2,1)} custom-call(bf16[256,256]{1,0:T(8,128)(2,1)} %get-tuple-element.21.left_ref.refs_1_, bf16[256,256]{1,0:T(8,128)(2,1)} %get-tuple-element.22.right_ref.refs_1_), custom_call_target="tpu_custom_call" | custom-call | tf_op jit(solution)/shard_map/order_posterior/pallas_call | solution.py:319
  (100 shorter events, 40.1 us)
Async XLA Ops:
  2.2 3.8 %collective-permute-start = (bf16[1,72,128]{2,1,0:T(8,128)(2,1)}, bf16[1,72,128]{2,1,0:T(8,128)(2,1)S(1)}, u32[]{:S(2)}, u32[]{:S(2)}) collective-permute-start(bf16[1,72,128]{2,1,0:T(8,128)(2,1)} %bitcast.27), channel_id=1, source_target_pairs={{0,4},{1,5},{2,6},{3,7},{4,0},{5,1},{6,2},{7,3},{8,12},{9,13},{10,... | collective-permute-start | bytes 55304 | tf_op jit(solution)/shard_map/ppermute | solution.py:57
  6.7 6.7 %collective-permute-start.1 = (bf16[2,72,128]{2,1,0:T(8,128)(2,1)S(1)}, bf16[2,72,128]{2,1,0:T(8,128)(2,1)S(1)}, u32[]{:S(2)}, u32[]{:S(2)}) collective-permute-start(bf16[2,72,128]{2,1,0:T(8,128)(2,1)S(1)} %pad_maximum_fusion.3), channel_id=1, source_target_pairs={{0,28},{1,29},{2,30},{3,31},{4,8},{5,9},{6,10},{7,11},{8,4},{9,5},... | collective-permute-start | bytes 110600 | tf_op jit(solution)/shard_map/ppermute | solution.py:57
  14.2 5.9 %collective-permute-start.2 = (bf16[4,72,128]{2,1,0:T(8,128)(2,1)S(1)}, bf16[4,72,128]{2,1,0:T(8,128)(2,1)S(1)}, u32[]{:S(2)}, u32[]{:S(2)}) collective-permute-start(bf16[4,72,128]{2,1,0:T(8,128)(2,1)S(1)} %pad_maximum_fusion.2.own_ref), channel_id=1, source_target_pairs={{0,12},{1,13},{2,14},{3,15},{4,24},{5,25},{6,26},{7,27},{8,20},{9,... | collective-permute-start | bytes 221192 | tf_op jit(solution)/shard_map/ppermute | solution.py:57
  23.5 5.6 %collective-permute-start.3 = (bf16[1,264,128]{2,1,0:T(8,128)(2,1)}, bf16[1,264,128]{2,1,0:T(8,128)(2,1)S(1)}, u32[]{:S(2)}, u32[]{:S(2)}) collective-permute-start(bf16[1,264,128]{2,1,0:T(8,128)(2,1)} %get-tuple-element.19), channel_id=1, source_target_pairs={{0,64},{1,65},{2,66},{3,67},{4,68},{5,69},{6,70},{7,71},{8,72},{9,... | collective-permute-start | bytes 202760 | tf_op jit(solution)/shard_map/ppermute | solution.py:49
  26.6 6.2 %collective-permute-start.9 = (bf16[2,264,128]{2,1,0:T(8,128)(2,1)S(1)}, bf16[2,264,128]{2,1,0:T(8,128)(2,1)S(1)}, u32[]{:S(2)}, u32[]{:S(2)}) collective-permute-start(bf16[2,264,128]{2,1,0:T(8,128)(2,1)S(1)} %pad_maximum_fusion.1), channel_id=1, source_target_pairs={{0,3},{1,2},{2,1},{3,0},{4,7},{5,6},{6,5},{7,4},{8,11},{9,10},{10,... | collective-permute-start | bytes 405512 | tf_op jit(solution)/shard_map/ppermute | solution.py:49
  30.0 7.0 %collective-permute-start.4 = (bf16[2,264,128]{2,1,0:T(8,128)(2,1)S(1)}, bf16[2,264,128]{2,1,0:T(8,128)(2,1)S(1)}, u32[]{:S(2)}, u32[]{:S(2)}) collective-permute-start(bf16[2,264,128]{2,1,0:T(8,128)(2,1)S(1)} %pad_maximum_fusion), channel_id=1, source_target_pairs={{0,96},{1,97},{2,98},{3,99},{4,100},{5,101},{6,102},{7,103},{8,104... | collective-permute-start | bytes 405512 | tf_op jit(solution)/shard_map/ppermute | solution.py:49
  32.9 6.4 %collective-permute-start.10 = (bf16[4,264,128]{2,1,0:T(8,128)(2,1)S(1)}, bf16[4,264,128]{2,1,0:T(8,128)(2,1)S(1)}, u32[]{:S(2)}, u32[]{:S(2)}) collective-permute-start(bf16[4,264,128]{2,1,0:T(8,128)(2,1)S(1)} %constant_dynamic-update-slice_fusion.3.b0), channel_id=1, source_target_pairs={{0,64},{1,65},{2,66},{3,67},{4,68},{5,69},{6,70},{7,71},{8,72},{9,... | collective-permute-start | bytes 811016 | tf_op jit(solution)/shard_map/ppermute | solution.py:49
  33.8 32.9 %collective-permute-start.11 = (bf16[4,264,128]{2,1,0:T(8,128)(2,1)S(1)}, bf16[4,264,128]{2,1,0:T(8,128)(2,1)S(1)}, u32[]{:S(2)}, u32[]{:S(2)}) collective-permute-start(bf16[4,264,128]{2,1,0:T(8,128)(2,1)S(1)} %constant_dynamic-update-slice_fusion.3.b0), channel_id=1, source_target_pairs={{0,96},{1,97},{2,98},{3,99},{4,100},{5,101},{6,102},{7,103},{8,104... | collective-permute-start | bytes 811016 | tf_op jit(solution)/shard_map/ppermute | solution.py:49
  35.8 30.9 %collective-permute-start.12 = (bf16[4,264,128]{2,1,0:T(8,128)(2,1)S(1)}, bf16[4,264,128]{2,1,0:T(8,128)(2,1)S(1)}, u32[]{:S(2)}, u32[]{:S(2)}) collective-permute-start(bf16[4,264,128]{2,1,0:T(8,128)(2,1)S(1)} %constant_dynamic-update-slice_fusion.3.b0), channel_id=1, source_target_pairs={{0,32},{1,33},{2,34},{3,35},{4,36},{5,37},{6,38},{7,39},{8,40},{9,... | collective-permute-start | bytes 811016 | tf_op jit(solution)/shard_map/ppermute | solution.py:49
  37.1 29.7 %collective-permute-start.5 = (bf16[4,264,128]{2,1,0:T(8,128)(2,1)S(1)}, bf16[4,264,128]{2,1,0:T(8,128)(2,1)S(1)}, u32[]{:S(2)}, u32[]{:S(2)}) collective-permute-start(bf16[4,264,128]{2,1,0:T(8,128)(2,1)S(1)} %constant_dynamic-update-slice_fusion.a0), channel_id=1, source_target_pairs={{0,1},{1,0},{2,3},{3,2},{4,5},{5,4},{6,7},{7,6},{8,9},{9,8},{10,11... | collective-permute-start | bytes 811016 | tf_op jit(solution)/shard_map/ppermute | solution.py:49
  37.2 29.6 %collective-permute-start.6 = (bf16[4,264,128]{2,1,0:T(8,128)(2,1)S(1)}, bf16[4,264,128]{2,1,0:T(8,128)(2,1)S(1)}, u32[]{:S(2)}, u32[]{:S(2)}) collective-permute-start(bf16[4,264,128]{2,1,0:T(8,128)(2,1)S(1)} %constant_dynamic-update-slice_fusion.a0), channel_id=1, source_target_pairs={{0,3},{1,2},{2,1},{3,0},{4,7},{5,6},{6,5},{7,4},{8,11},{9,10},{10,... | collective-permute-start | bytes 811016 | tf_op jit(solution)/shard_map/ppermute | solution.py:49
  39.3 27.5 %collective-permute-start.7 = (bf16[4,264,128]{2,1,0:T(8,128)(2,1)S(1)}, bf16[4,264,128]{2,1,0:T(8,128)(2,1)S(1)}, u32[]{:S(2)}, u32[]{:S(2)}) collective-permute-start(bf16[4,264,128]{2,1,0:T(8,128)(2,1)S(1)} %constant_dynamic-update-slice_fusion.a0), channel_id=1, source_target_pairs={{0,2},{1,3},{2,0},{3,1},{4,6},{5,7},{6,4},{7,5},{8,10},{9,11},{10,... | collective-permute-start | bytes 811016 | tf_op jit(solution)/shard_map/ppermute | solution.py:49
  94.7 14.7 %collective-permute-start.18 = (bf16[4,264,128]{2,1,0:T(8,128)(2,1)}, bf16[4,264,128]{2,1,0:T(8,128)(2,1)S(1)}, u32[]{:S(2)}, u32[]{:S(2)}) collective-permute-start(bf16[4,264,128]{2,1,0:T(8,128)(2,1)} %get-tuple-element.28), channel_id=1, source_target_pairs={{0,64},{1,65},{2,66},{3,67},{4,68},{5,69},{6,70},{7,71},{8,72},{9,... | collective-permute-start | bytes 811016 | tf_op jit(solution)/shard_map/ppermute | solution.py:49
  95.3 15.5 %collective-permute-start.19 = (bf16[4,264,128]{2,1,0:T(8,128)(2,1)}, bf16[4,264,128]{2,1,0:T(8,128)(2,1)S(1)}, u32[]{:S(2)}, u32[]{:S(2)}) collective-permute-start(bf16[4,264,128]{2,1,0:T(8,128)(2,1)} %get-tuple-element.29), channel_id=1, source_target_pairs={{0,96},{1,97},{2,98},{3,99},{4,100},{5,101},{6,102},{7,103},{8,104... | collective-permute-start | bytes 811016 | tf_op jit(solution)/shard_map/ppermute | solution.py:49
  97.2 13.6 %collective-permute-start.20 = (bf16[4,264,128]{2,1,0:T(8,128)(2,1)}, bf16[4,264,128]{2,1,0:T(8,128)(2,1)S(1)}, u32[]{:S(2)}, u32[]{:S(2)}) collective-permute-start(bf16[4,264,128]{2,1,0:T(8,128)(2,1)} %get-tuple-element.30), channel_id=1, source_target_pairs={{0,32},{1,33},{2,34},{3,35},{4,36},{5,37},{6,38},{7,39},{8,40},{9,... | collective-permute-start | bytes 811016 | tf_op jit(solution)/shard_map/ppermute | solution.py:49
  107.4 5.9 %collective-permute-start.13 = (bf16[4,264,128]{2,1,0:T(8,128)(2,1)}, bf16[4,264,128]{2,1,0:T(8,128)(2,1)S(1)}, u32[]{:S(2)}, u32[]{:S(2)}) collective-permute-start(bf16[4,264,128]{2,1,0:T(8,128)(2,1)} %get-tuple-element.24), channel_id=1, source_target_pairs={{0,1},{1,0},{2,3},{3,2},{4,5},{5,4},{6,7},{7,6},{8,9},{9,8},{10,11... | collective-permute-start | bytes 811016 | tf_op jit(solution)/shard_map/ppermute | solution.py:49
  108.0 9.6 %collective-permute-start.14 = (bf16[4,264,128]{2,1,0:T(8,128)(2,1)}, bf16[4,264,128]{2,1,0:T(8,128)(2,1)S(1)}, u32[]{:S(2)}, u32[]{:S(2)}) collective-permute-start(bf16[4,264,128]{2,1,0:T(8,128)(2,1)} %get-tuple-element.25), channel_id=1, source_target_pairs={{0,3},{1,2},{2,1},{3,0},{4,7},{5,6},{6,5},{7,4},{8,11},{9,10},{10,... | collective-permute-start | bytes 811016 | tf_op jit(solution)/shard_map/ppermute | solution.py:49
  109.4 8.2 %collective-permute-start.15 = (bf16[4,264,128]{2,1,0:T(8,128)(2,1)}, bf16[4,264,128]{2,1,0:T(8,128)(2,1)S(1)}, u32[]{:S(2)}, u32[]{:S(2)}) collective-permute-start(bf16[4,264,128]{2,1,0:T(8,128)(2,1)} %get-tuple-element.26), channel_id=1, source_target_pairs={{0,2},{1,3},{2,0},{3,1},{4,6},{5,7},{6,4},{7,5},{8,10},{9,11},{10,... | collective-permute-start | bytes 811016 | tf_op jit(solution)/shard_map/ppermute | solution.py:49
  110.9 9.0 %collective-permute-start.21 = (bf16[2,264,128]{2,1,0:T(8,128)(2,1)S(1)}, bf16[2,264,128]{2,1,0:T(8,128)(2,1)S(1)}, u32[]{:S(2)}, u32[]{:S(2)}) collective-permute-start(bf16[2,264,128]{2,1,0:T(8,128)(2,1)S(1)} %slice.78), channel_id=1, source_target_pairs={{0,3},{1,2},{2,1},{3,0},{4,7},{5,6},{6,5},{7,4},{8,11},{9,10},{10,... | collective-permute-start | bytes 405512 | tf_op jit(solution)/shard_map/ppermute | solution.py:49
  117.8 5.5 %collective-permute-start.16 = (bf16[2,264,128]{2,1,0:T(8,128)(2,1)S(1)}, bf16[2,264,128]{2,1,0:T(8,128)(2,1)S(1)}, u32[]{:S(2)}, u32[]{:S(2)}) collective-permute-start(bf16[2,264,128]{2,1,0:T(8,128)(2,1)S(1)} %slice.79), channel_id=1, source_target_pairs={{0,96},{1,97},{2,98},{3,99},{4,100},{5,101},{6,102},{7,103},{8,104... | collective-permute-start | bytes 405512 | tf_op jit(solution)/shard_map/ppermute | solution.py:49
  120.0 4.7 %collective-permute-start.22 = (bf16[1,264,128]{2,1,0:T(8,128)(2,1)S(1)}, bf16[1,264,128]{2,1,0:T(8,128)(2,1)S(1)}, u32[]{:S(2)}, u32[]{:S(2)}) collective-permute-start(bf16[1,264,128]{2,1,0:T(8,128)(2,1)S(1)} %slice.80), channel_id=1, source_target_pairs={{0,1},{1,0},{2,3},{3,2},{4,5},{5,4},{6,7},{7,6},{8,9},{9,8},{10,11... | collective-permute-start | bytes 202760 | tf_op jit(solution)/shard_map/ppermute | solution.py:49
  129.2 6.0 %collective-permute-start.23 = (bf16[4,72,128]{2,1,0:T(8,128)(2,1)}, bf16[4,72,128]{2,1,0:T(8,128)(2,1)S(1)}, u32[]{:S(2)}, u32[]{:S(2)}) collective-permute-start(bf16[4,72,128]{2,1,0:T(8,128)(2,1)} %get-tuple-element.32), channel_id=1, source_target_pairs={{0,12},{1,13},{2,14},{3,15},{4,24},{5,25},{6,26},{7,27},{8,20},{9,... | collective-permute-start | bytes 221192 | tf_op jit(solution)/shard_map/ppermute | solution.py:57
  136.1 4.1 %collective-permute-start.24 = (bf16[2,72,128]{2,1,0:T(8,128)(2,1)S(1)}, bf16[2,72,128]{2,1,0:T(8,128)(2,1)S(1)}, u32[]{:S(2)}, u32[]{:S(2)}) collective-permute-start(bf16[2,72,128]{2,1,0:T(8,128)(2,1)S(1)} %slice.82), channel_id=1, source_target_pairs={{0,28},{1,29},{2,30},{3,31},{4,8},{5,9},{6,10},{7,11},{8,4},{9,5},... | collective-permute-start | bytes 110600 | tf_op jit(solution)/shard_map/ppermute | solution.py:57
  143.6 17.4 %collective-permute-start.26 = (bf16[72,128]{1,0:T(8,128)(2,1)S(1)}, bf16[72,128]{1,0:T(8,128)(2,1)S(1)}, u32[]{:S(2)}, u32[]{:S(2)}) collective-permute-start(bf16[72,128]{1,0:T(8,128)(2,1)S(1)} %get-tuple-element.35), channel_id=1, source_target_pairs={{0,128},{128,0},{1,129},{129,1},{2,130},{130,2},{3,131},{131,3},{4... | collective-permute-start | bytes 55304 | tf_op jit(solution)/shard_map/ppermute | solution.py:591
  (18 other events, 84.8 us)
where the time goes:
time: 164 us; the launch traced here: 163 us
  Pallas kernels  67.6 us (41%)
  starting transfers between devices  53.7 us (33%)
  waiting for transfers between devices  26.7 us (16%)
  other arithmetic  8.24 us (5%)
  local copies, waits for them, and re-layouts  5.28 us (3%)
    ppermute x20, starting transfers between devices, trade(): return lax.ppermute(value, PAIR, pairs)  25.7 us
    pallas_call x4, Pallas kernels, weight_images(): pl.pallas_call(weight_kernel, grid=(count,), in_specs=[pl.BlockSpec((1, N...  23 us
    pallas_call x2, Pallas kernels, project_back(): pl.pallas_call(kernel, in_specs=[SMEM, VMEM] + [ANY] * 4 + [VMEM] * 2, ou...  18.8 us
    pallas_call x1, Pallas kernels, score(): pl.pallas_call(score_kernel, in_specs=[SMEM] + [VMEM] * 8 + [ANY] * 4 + [...  17.5 us
    ppermute x6, waiting for transfers between devices, trade_z(): return lax.ppermute(value, PAIR, pairs)  16.6 us
    ppermute x1, starting transfers between devices, run(): partner = lax.ppermute(own.astype(jnp.bfloat16), 'half', [(0, 1), (1, 0)])  15.4 us
    ppermute x6, starting transfers between devices, trade_z(): return lax.ppermute(value, PAIR, pairs)  12.6 us
    ppermute x20, waiting for transfers between devices, trade(): return lax.ppermute(value, PAIR, pairs)  10.1 us
  transfers between devices with their start and end apart: 27, of which 10 were waited for; matrix products, arithmetic and copies ran while one was open for 5% of the time, Pallas kernels for 21%

commit v1 on v0

--- a/solution.py
+++ b/solution.py
@@ -20,7 +20,7 @@
 TILES = FC // LANE
 CHUNK = 640
 STEPS = FC // CHUNK
-PARTS = (3, 3, 3, 4)
+PART = 1664
 ROWS = 264
 NX, NY, NZ = 4, 4, 8
 GRAY = (0, 1, 3, 2)
@@ -144,7 +144,7 @@
         for c in range(2):
             value = image_ref[0, rows, c, :].astype(jnp.float32)
             value = (ctf_ref[rows, :] * value).astype(jnp.bfloat16)
-            for tile in range(CHUNK // LANE):
+            for tile in range(PART // LANE):
                 start = (2 * tile + c) * LANE
                 out_ref[rows, start : start + LANE] = value[:, tile * LANE : (tile + 1) * LANE]
         return carry
@@ -152,38 +152,29 @@
     lax.fori_loop(0, NP // 16, body, 0)
 
 
-def weight_images(part, images, table, group_row):
-    first, count = sum(PARTS[:part]), PARTS[part]
+def weight_images(images, table, group_row):
     return pl.pallas_call(
         weight_kernel,
-        grid=(count,),
+        grid=(FC // PART,),
         in_specs=[
-            pl.BlockSpec((1, NP, 2, CHUNK), lambda j: (0, 0, 0, first + j)),
-            pl.BlockSpec((1, G, CHUNK), lambda j: (0, 0, first + j)),
+            pl.BlockSpec((1, NP, 2, PART), lambda j: (0, 0, 0, j)),
+            pl.BlockSpec((1, G, PART), lambda j: (0, 0, j)),
             pl.BlockSpec((1, NP), lambda j: (0, 0)),
         ],
-        out_specs=pl.BlockSpec((NP, 2 * CHUNK), lambda j: (0, j)),
-        out_shape=jax.ShapeDtypeStruct((NP, 2 * CHUNK * count), jnp.bfloat16),
+        out_specs=pl.BlockSpec((NP, 2 * PART), lambda j: (0, j)),
+        out_shape=jax.ShapeDtypeStruct((NP, 2 * FC), jnp.bfloat16),
         scratch_shapes=[
-            pltpu.VMEM((NP, CHUNK), jnp.float32),
+            pltpu.VMEM((NP, PART), jnp.float32),
             pltpu.VMEM((NP, 3 * G), jnp.bfloat16),
         ],
         compiler_params=pltpu.CompilerParams(vmem_limit_bytes=VMEM_LIMIT),
+        name="weight_images",
     )(images, table, group_row)
 
 
-def start_copies(w_hbms, w_ref, sem_ref):
-    step = 0
-    for part, count in enumerate(PARTS):
-        for n in range(count):
-            lanes = slice(n * 2 * CHUNK, (n + 1) * 2 * CHUNK)
-            pltpu.make_async_copy(w_hbms[part].at[:, lanes], w_ref.at[step], sem_ref.at[step]).start()
-            step += 1
-
-
-def wait_copy(w_hbms, w_ref, sem_ref, step):
-    source = w_hbms[0].at[:, 0 : 2 * CHUNK]
-    pltpu.make_async_copy(source, w_ref.at[step], sem_ref.at[step]).wait()
+def weight_copy(w_hbm, w_ref, sem_ref, step):
+    lanes = pl.ds(pl.multiple_of(step * (2 * CHUNK), LANE), 2 * CHUNK)
+    return pltpu.make_async_copy(w_hbm.at[:, lanes], w_ref.at[step], sem_ref.at[step])
 
 
 def unpack_sections(pos_ref, a_refs, b_refs, nat_ref, ex_ref):
@@ -224,12 +215,12 @@
 
 
 def score_kernel(
-    pos_ref, a0, a1, a2, a3, b0, b1, b2, b3, w0, w1, w2, w3, table_ref, inv_ref,
-    cos_ref, sin_ref, group_ref, orient_ref, left_ref, right_ref,
-    nat_ref, ex_ref, shift_ref, acc_ref, norm_ref, w_ref, sem_ref,
+    pos_ref, a0, a1, a2, a3, b0, b1, b2, b3, w_hbm, table_ref, inv_ref,
+    cos_ref, sin_ref, group_ref, orient_ref, left_ref, right_ref, p0, p1, p2, p3,
+    nat_ref, ex_ref, shift_ref, acc_ref, norm_ref, w_ref, sem_ref, slab_ref, sum_ref,
 ):
-    w_hbms = (w0, w1, w2, w3)
-    start_copies(w_hbms, w_ref, sem_ref)
+    for step in range(STEPS):
+        weight_copy(w_hbm, w_ref, sem_ref, step).start()
     unpack_sections(pos_ref, (a0, a1, a2, a3), (b0, b1, b2, b3), nat_ref, ex_ref)
     acc_ref[...] = jnp.zeros_like(acc_ref)
     norm_ref[...] = jnp.zeros_like(norm_ref)
@@ -268,8 +259,8 @@
     shift(0, 0)
 
     def body(j, carry):
-        wait_copy(w_hbms, w_ref, sem_ref, 2 * j)
-        wait_copy(w_hbms, w_ref, sem_ref, 2 * j + 1)
+        weight_copy(w_hbm, w_ref, sem_ref, 2 * j).wait()
+        weight_copy(w_hbm, w_ref, sem_ref, 2 * j + 1).wait()
         shift(2 * j + 1, 1)
         multiply(2 * j, 0)
         shift(2 * j + 2, 0)
@@ -277,7 +268,7 @@
         return carry
 
     lax.fori_loop(0, STEPS // 2, body, 0)
-    wait_copy(w_hbms, w_ref, sem_ref, STEPS - 1)
+    weight_copy(w_hbm, w_ref, sem_ref, STEPS - 1).wait()
     multiply(STEPS - 1, 0)
 
     wide = K * TR * O
@@ -300,6 +291,10 @@
         for color, out in ((0, left_ref), (1, right_ref)):
             k = cls * 4 + color * 2
             out[cls * 128 : cls * 128 + 128, :] = rounded[k * 64 : k * 64 + 128, :]
+    back_body(
+        0, pos_ref, left_ref, w_ref, lambda step: None, cos_ref, sin_ref, (p0, p1, p2, p3),
+        slab_ref, sum_ref, ex_ref,
+    )
 
 
 def order_kernel(left_ref, right_ref, post_ref):
@@ -332,8 +327,8 @@
     wide = K * O * TR
     return pl.pallas_call(
         score_kernel,
-        in_specs=[SMEM] + [VMEM] * 8 + [ANY] * 4 + [VMEM] * 6,
-        out_specs=[VMEM] * 2,
+        in_specs=[SMEM] + [VMEM] * 8 + [ANY] + [VMEM] * 6,
+        out_specs=[VMEM] * 6,
         scratch_shapes=[
             pltpu.VMEM((128, FC), jnp.float32),
             pltpu.VMEM((256, LANE), jnp.float32),
@@ -342,23 +337,22 @@
             pltpu.VMEM((K * O, G), jnp.float32),
             pltpu.VMEM((STEPS, NP, 2 * CHUNK), jnp.bfloat16),
             pltpu.SemaphoreType.DMA((STEPS,)),
+            pltpu.VMEM((64, FC), jnp.float32),
+            pltpu.VMEM((2, NP, 2 * CHUNK), jnp.float32),
         ],
         out_shape=[
             jax.ShapeDtypeStruct((wide // 2, NP), jnp.bfloat16),
             jax.ShapeDtypeStruct((wide // 2, NP), jnp.bfloat16),
-        ],
+        ]
+        + [jax.ShapeDtypeStruct((4, ROWS, LANE), jnp.bfloat16)] * 4,
         compiler_params=pltpu.CompilerParams(vmem_limit_bytes=VMEM_LIMIT),
         name="score",
-    )(pos, *a, *b, *weighted, table, inverse, cosine, sine, group_row, orient)
-
-
-def back_kernel(
-    color, pos_ref, post_ref, w0, w1, w2, w3, cos_ref, sin_ref, p0, p1, p2, p3,
-    slab_ref, sum_ref, ex_ref, w_ref, sem_ref,
+    )(pos, *a, *b, weighted, table, inverse, cosine, sine, group_row, orient)
+
+
+def back_body(
+    color, pos_ref, post_ref, w_ref, wait, cos_ref, sin_ref, outs, slab_ref, sum_ref, ex_ref
 ):
-    w_hbms = (w0, w1, w2, w3)
-    start_copies(w_hbms, w_ref, sem_ref)
-
     def multiply(step, slot):
         sum_ref[slot] = mm(post_ref[...], w_ref[step])
 
@@ -379,12 +373,12 @@
                     imag * cosine - real * sine, axis=0
                 )
 
-    wait_copy(w_hbms, w_ref, sem_ref, 0)
+    wait(0)
     multiply(0, 0)
 
     def body(j, carry):
-        wait_copy(w_hbms, w_ref, sem_ref, 2 * j + 1)
-        wait_copy(w_hbms, w_ref, sem_ref, 2 * j + 2)
+        wait(2 * j + 1)
+        wait(2 * j + 2)
         multiply(2 * j + 1, 1)
         combine(2 * j, 0)
         multiply(2 * j + 2, 0)
@@ -408,7 +402,7 @@
             spread = (iota((32, LANE), 1) == 2 * iota((32, LANE), 0) + u).astype(jnp.float32)
             total += mm(column.astype(jnp.bfloat16), spread.astype(jnp.bfloat16))
         ex_ref[cls * 64 : cls * 64 + 64, :] = total
-    for near, out in enumerate((p0, p1, p2, p3)):
+    for near, out in enumerate(outs):
 
         def pack(far, carry, near=near, out=out):
             cls, chunks = sources(pos_ref, near, far, color)
@@ -427,13 +421,26 @@
         lax.fori_loop(0, 4, pack, 0)
 
 
-def project_back(color, pos, post, weighted, cosine, sine):
-    def kernel(*refs):
-        back_kernel(color, *refs)
-
+def back_kernel(
+    pos_ref, post_ref, w_hbm, cos_ref, sin_ref, p0, p1, p2, p3,
+    slab_ref, sum_ref, ex_ref, w_ref, sem_ref,
+):
+    for step in range(STEPS):
+        weight_copy(w_hbm, w_ref, sem_ref, step).start()
+
+    def wait(step):
+        weight_copy(w_hbm, w_ref, sem_ref, step).wait()
+
+    back_body(
+        1, pos_ref, post_ref, w_ref, wait, cos_ref, sin_ref, (p0, p1, p2, p3),
+        slab_ref, sum_ref, ex_ref,
+    )
+
+
+def project_back(pos, post, weighted, cosine, sine):
     return pl.pallas_call(
-        kernel,
-        in_specs=[SMEM, VMEM] + [ANY] * 4 + [VMEM] * 2,
+        back_kernel,
+        in_specs=[SMEM, VMEM, ANY] + [VMEM] * 2,
         out_specs=[VMEM] * 4,
         scratch_shapes=[
             pltpu.VMEM((64, FC), jnp.float32),
@@ -444,7 +451,8 @@
         ],
         out_shape=[jax.ShapeDtypeStruct((4, ROWS, LANE), jnp.bfloat16)] * 4,
         compiler_params=pltpu.CompilerParams(vmem_limit_bytes=VMEM_LIMIT),
-    )(pos, post, *weighted, cosine, sine)
+        name="project_back",
+    )(pos, post, weighted, cosine, sine)
 
 
 def finish_kernel(own_ref, partner_ref, slab_ref, product_ref):
@@ -549,9 +557,7 @@
         [img % 4, 2 * (img // 32) + cls, (img // 4) % 8, counts[0, 0]]
     ).astype(jnp.int32)
     cosine, sine = phases(trans_ids[0], FC)
-    weighted = []
-    for part in range(len(PARTS)):
-        weighted.append(weight_images(part, images, ctf_table, ctf_group))
+    weighted = weight_images(images, ctf_table, ctf_group)
 
     along = pack_sections(projections)[None]
     for odd in (-1, 1):
@@ -567,13 +573,12 @@
     for mask in GRAY[1:]:
         rights.append(trade(right, my=mask))
 
-    post_left, post_right = score(
+    post_left, post_right, *pieces = score(
         pos, lefts, rights, weighted, ctf_table, inv_sigma, cosine, sine, ctf_group, orient_ids[0].T
     )
 
-    pieces = project_back(0, pos, post_left, weighted, cosine, sine)
     left = added([pieces[0]] + [trade(pieces[d], mx=GRAY[d]) for d in range(1, 4)])
-    pieces = project_back(1, pos, post_right, weighted, cosine, sine)
+    pieces = project_back(pos, post_right, weighted, cosine, sine)
     parts = [pieces[0]]
     for d in range(1, 4):
         parts.append(trade(pieces[d], my=GRAY[d]))
@@ -583,7 +588,7 @@
     right = added([right[:2], trade(right[2:].astype(jnp.bfloat16), mx=3)])
     left_got = trade(left[1:].astype(jnp.bfloat16), my=1)
     right_got = trade(right[1:].astype(jnp.bfloat16), mx=1)
-    own, sent = ungroup(left[:1], left_got, right[:1], right_got)
+    own, sent = ungroup(left, left_got, right, right_got)
     own = own + trade_z(sent, -3).astype(jnp.float32)
     for odd, size in ((1, 2), (-1, 1)):
         own = added([own[:size], trade_z(own[size:].astype(jnp.bfloat16), odd)])

time: 164 us -> 152 us (0.927)
  Pallas kernels: 67.6 us -> 54.5 us
  waiting for transfers between devices: 26.7 us -> 29.5 us
    pallas_call x7 -> x3, Pallas kernels: 59.2 us -> 46.1 us  [the longest x1 23.9 us: score(): pl.pallas_call(score_kernel, in_specs=[SMEM] + [VMEM] * 8 + [ANY] + [VMEM...]
    ppermute x20, waiting for transfers between devices: 10.1 us -> 13 us  [trade(): return lax.ppermute(value, PAIR, pairs)]
    unnamed x33 -> x35, local copies, waits for them, and re-layouts: 3.84 us -> 3.82 us
  transfers between devices with their start and end apart: 27 -> 27, of which waited for: 10 -> 14; matrix products, arithmetic and copies ran while one was open for 5% -> 5% of each run, Pallas kernels for 21% -> 16%
where the time goes in v1:
time: 152 us; the launch traced here: 151 us
  Pallas kernels  54.5 us (36%)
  starting transfers between devices  52.5 us (35%)
  waiting for transfers between devices  29.5 us (19%)
  other arithmetic  9.21 us (6%)
  local copies, waits for them, and re-layouts  3.94 us (3%)
  between operations  1.6 us (1%)
    ppermute x20, starting transfers between devices, trade(): return lax.ppermute(value, PAIR, pairs)  24.4 us
    pallas_call x1, Pallas kernels, score(): pl.pallas_call(score_kernel, in_specs=[SMEM] + [VMEM] * 8 + [ANY] + [VMEM...  23.9 us
    ppermute x6, waiting for transfers between devices, trade_z(): return lax.ppermute(value, PAIR, pairs)  16.5 us
    ppermute x1, starting transfers between devices, run(): partner = lax.ppermute(own.astype(jnp.bfloat16), 'half', [(0, 1), (1, 0)])  15.3 us
    ppermute x20, waiting for transfers between devices, trade(): return lax.ppermute(value, PAIR, pairs)  13 us
    pallas_call x1, Pallas kernels, weight_images(): pl.pallas_call(weight_kernel, grid=(FC // PART,), in_specs=[pl.BlockSpec(...  12.8 us
    ppermute x6, starting transfers between devices, trade_z(): return lax.ppermute(value, PAIR, pairs)  12.7 us
    pallas_call x1, Pallas kernels, project_back(): pl.pallas_call(back_kernel, in_specs=[SMEM, VMEM, ANY] + [VMEM] * 2, out_...  9.37 us
  transfers between devices with their start and end apart: 27, of which 14 were waited for; matrix products, arithmetic and copies ran while one was open for 5% of the time, Pallas kernels for 16%

profile of v1, /device:TPU:1, one launch (start us, length us, event | category | flops | bytes accessed | tf_op | source)
XLA Modules:
  0.0 151.3 jit_solution(17533148255121203145)
XLA Ops:
  2.2 2.5 %collective-permute-start = (bf16[1,72,128]{2,1,0:T(8,128)(2,1)}, bf16[1,72,128]{2,1,0:T(8,128)(2,1)S(1)}, u32[]{:S(2)}, u32[]{:S(2)}) collective-permute-start(bf16[1,72,128]{2,1,0:T(8,128)(2,1)} %bitcast.27), channel_id=1, source_target_pairs={{0,4},{1,5},{2,6},{3,7},{4,0},{5,1},{6,2},{7,3},{8,12},{9,13},{10,... | collective-permute-start | bytes 55304 | tf_op jit(solution)/shard_map/ppermute | solution.py:57
  6.7 5.4 %collective-permute-start.1 = (bf16[2,72,128]{2,1,0:T(8,128)(2,1)S(1)}, bf16[2,72,128]{2,1,0:T(8,128)(2,1)S(1)}, u32[]{:S(2)}, u32[]{:S(2)}) collective-permute-start(bf16[2,72,128]{2,1,0:T(8,128)(2,1)S(1)} %pad_maximum_fusion.3), channel_id=1, source_target_pairs={{0,28},{1,29},{2,30},{3,31},{4,8},{5,9},{6,10},{7,11},{8,4},{9,5},... | collective-permute-start | bytes 110600 | tf_op jit(solution)/shard_map/ppermute | solution.py:57
  15.9 4.1 %collective-permute-done.2.got_ref = bf16[4,72,128]{2,1,0:T(8,128)(2,1)S(1)} collective-permute-done((bf16[4,72,128]{2,1,0:T(8,128)(2,1)S(1)}, bf16[4,72,128]{2,1,0:T(8,128)(2,1)S(1)}, u32[]{:S(2)}, u32[]{:S(2)}) %collective-permute-start.2) | collective-permute-done | bytes 73760 | tf_op jit(solution)/shard_map/ppermute | solution.py:57
  27.8 2.6 %collective-permute-start.9 = (bf16[2,264,128]{2,1,0:T(8,128)(2,1)S(1)}, bf16[2,264,128]{2,1,0:T(8,128)(2,1)S(1)}, u32[]{:S(2)}, u32[]{:S(2)}) collective-permute-start(bf16[2,264,128]{2,1,0:T(8,128)(2,1)S(1)} %pad_maximum_fusion.1), channel_id=1, source_target_pairs={{0,3},{1,2},{2,1},{3,0},{4,7},{5,6},{6,5},{7,4},{8,11},{9,10},{10,... | collective-permute-start | bytes 405512 | tf_op jit(solution)/shard_map/ppermute | solution.py:49
  31.3 2.0 %collective-permute-start.4 = (bf16[2,264,128]{2,1,0:T(8,128)(2,1)S(1)}, bf16[2,264,128]{2,1,0:T(8,128)(2,1)S(1)}, u32[]{:S(2)}, u32[]{:S(2)}) collective-permute-start(bf16[2,264,128]{2,1,0:T(8,128)(2,1)S(1)} %pad_maximum_fusion), channel_id=1, source_target_pairs={{0,96},{1,97},{2,98},{3,99},{4,100},{5,101},{6,102},{7,103},{8,104... | collective-permute-start | bytes 405512 | tf_op jit(solution)/shard_map/ppermute | solution.py:49
  33.4 2.4 %collective-permute-start.12 = (bf16[4,264,128]{2,1,0:T(8,128)(2,1)S(1)}, bf16[4,264,128]{2,1,0:T(8,128)(2,1)S(1)}, u32[]{:S(2)}, u32[]{:S(2)}) collective-permute-start(bf16[4,264,128]{2,1,0:T(8,128)(2,1)S(1)} %constant_dynamic-update-slice_fusion.3.b0), channel_id=1, source_target_pairs={{0,32},{1,33},{2,34},{3,35},{4,36},{5,37},{6,38},{7,39},{8,40},{9,... | collective-permute-start | bytes 811016 | tf_op jit(solution)/shard_map/ppermute | solution.py:49
  40.3 1.9 %fusion = (f32[8,8320]{1,0:T(8,128)}, f32[8,8320]{1,0:T(8,128)}) fusion(f32[8320]{0:T(1024)S(1)} %get-tuple-element.43, f32[8]{0:T(128)S(1)} %get-tuple-element.40, f32[8320]{0:T(1024)S(1)} %get-tuple-element.44, f32[8]{0:T(128)S(1)} %get-tuple-element.39), kind=kLoop, calls=%fused_computation.7 | loop fusion | flops 266240 | bytes 599104 | tf_op jit(solution)/shard_map/sin | solution.py:84
  42.8 12.8 %weight_images.1.w_hbm = bf16[256,16640]{1,0:T(8,128)(2,1)} custom-call(bf16[1,256,2,8320]{3,2,1,0:T(2,128)(2,1)} %image_ref.1, f32[1,32,8320]{2,1,0:T(8,128)} %table_ref.3, s32[1,256]{1,0:T(1,128)} %group_ref.3), custom_call_target="tpu_custom_call" | custom-call | tf_op jit(solution)/shard_map/weight_images/pallas_call | solution.py:156
  57.3 23.9 %score.1 = (bf16[256,256]{1,0:T(8,128)(2,1)}, bf16[256,256]{1,0:T(8,128)(2,1)}, bf16[4,264,128]{2,1,0:T(8,128)(2,1)}, bf16[4,264,128]{2,1,0:T(8,128)(2,1)}, bf16...) custom-call(s32[4]{0:T(128)} %pad_add_fusion.pos_ref, bf16[4,264,128]{2,1,0:T(8,128)(2,1)} %copy-done.2, ...), custom_call_target="tpu_custom_call" | custom-call | tf_op jit(solution)/shard_map/score/pallas_call | solution.py:328
  82.7 2.2 %collective-permute-start.14 = (bf16[4,264,128]{2,1,0:T(8,128)(2,1)}, bf16[4,264,128]{2,1,0:T(8,128)(2,1)S(1)}, u32[]{:S(2)}, u32[]{:S(2)}) collective-permute-start(bf16[4,264,128]{2,1,0:T(8,128)(2,1)} %get-tuple-element.25), channel_id=1, source_target_pairs={{0,3},{1,2},{2,1},{3,0},{4,7},{5,6},{6,5},{7,4},{8,11},{9,10},{10,... | collective-permute-start | bytes 811016 | tf_op jit(solution)/shard_map/ppermute | solution.py:49
  85.0 9.4 %project_back.1 = (bf16[4,264,128]{2,1,0:T(8,128)(2,1)}, bf16[4,264,128]{2,1,0:T(8,128)(2,1)}, bf16[4,264,128]{2,1,0:T(8,128)(2,1)}, bf16[4,264,128]{2,1,0:T(8,128)(2,1)}) custom-call(s32[4]{0:T(128)} %pad_add_fusion.pos_ref, bf16[256,256]{1,0:T(8,128)(2,1)} %get-tuple-element.22.right_ref.post_ref, bf16[256,16640]{1,0:T(8,128)(2,1)} %weight_images.1.w_hbm, ...), custom_call_target="tpu_custom_call" | custom-call | tf_op jit(solution)/shard_map/project_back/pallas_call | solution.py:441
  95.3 2.6 %collective-permute-start.19 = (bf16[4,264,128]{2,1,0:T(8,128)(2,1)}, bf16[4,264,128]{2,1,0:T(8,128)(2,1)S(1)}, u32[]{:S(2)}, u32[]{:S(2)}) collective-permute-start(bf16[4,264,128]{2,1,0:T(8,128)(2,1)} %get-tuple-element.29), channel_id=1, source_target_pairs={{0,96},{1,97},{2,98},{3,99},{4,100},{5,101},{6,102},{7,103},{8,104... | collective-permute-start | bytes 811016 | tf_op jit(solution)/shard_map/ppermute | solution.py:49
  98.0 2.2 %collective-permute-start.16 = (bf16[2,264,128]{2,1,0:T(8,128)(2,1)S(1)}, bf16[2,264,128]{2,1,0:T(8,128)(2,1)S(1)}, u32[]{:S(2)}, u32[]{:S(2)}) collective-permute-start(bf16[2,264,128]{2,1,0:T(8,128)(2,1)S(1)} %slice.69), channel_id=1, source_target_pairs={{0,96},{1,97},{2,98},{3,99},{4,100},{5,101},{6,102},{7,103},{8,104... | collective-permute-start | bytes 405512 | tf_op jit(solution)/shard_map/ppermute | solution.py:49
  100.3 4.2 %collective-permute-done.19 = bf16[4,264,128]{2,1,0:T(8,128)(2,1)S(1)} collective-permute-done((bf16[4,264,128]{2,1,0:T(8,128)(2,1)}, bf16[4,264,128]{2,1,0:T(8,128)(2,1)S(1)}, u32[]{:S(2)}, u32[]{:S(2)}) %collective-permute-start.19) | collective-permute-done | bytes 270368 | tf_op jit(solution)/shard_map/ppermute | solution.py:49
  106.1 1.9 %collective-permute-start.21 = (bf16[2,264,128]{2,1,0:T(8,128)(2,1)S(1)}, bf16[2,264,128]{2,1,0:T(8,128)(2,1)S(1)}, u32[]{:S(2)}, u32[]{:S(2)}) collective-permute-start(bf16[2,264,128]{2,1,0:T(8,128)(2,1)S(1)} %slice.68), channel_id=1, source_target_pairs={{0,3},{1,2},{2,1},{3,0},{4,7},{5,6},{6,5},{7,4},{8,11},{9,10},{10,... | collective-permute-start | bytes 405512 | tf_op jit(solution)/shard_map/ppermute | solution.py:49
  108.6 2.8 %collective-permute-done.21 = bf16[2,264,128]{2,1,0:T(8,128)(2,1)S(1)} collective-permute-done((bf16[2,264,128]{2,1,0:T(8,128)(2,1)S(1)}, bf16[2,264,128]{2,1,0:T(8,128)(2,1)S(1)}, u32[]{:S(2)}, u32[]{:S(2)}) %collective-permute-start.21) | collective-permute-done | bytes 135200 | tf_op jit(solution)/shard_map/ppermute | solution.py:49
  112.2 2.8 %collective-permute-done.22.r1_ref = bf16[1,264,128]{2,1,0:T(8,128)(2,1)S(1)} collective-permute-done((bf16[1,264,128]{2,1,0:T(8,128)(2,1)S(1)}, bf16[1,264,128]{2,1,0:T(8,128)(2,1)S(1)}, u32[]{:S(2)}, u32[]{:S(2)}) %collective-permute-start.22) | collective-permute-done | bytes 67616 | tf_op jit(solution)/shard_map/ppermute | solution.py:49
  115.6 1.8 %ungroup.1 = (f32[4,72,128]{2,1,0:T(8,128)}, bf16[4,72,128]{2,1,0:T(8,128)(2,1)}) custom-call(f32[2,264,128]{2,1,0:T(8,128)} %copy-done, bf16[1,264,128]{2,1,0:T(8,128)(2,1)} %copy-done.13, f32[2,264,128]{2,1,0:T(8,128)} %copy-done.1, bf16[1,264,128]{2,1,0:T(8,128)(2,1)} %copy-done.14), custom_call_target="tpu_custom_call" | custom-call | tf_op jit(solution)/shard_map/ungroup/pallas_call | solution.py:537
  117.4 1.7 %collective-permute-start.23 = (bf16[4,72,128]{2,1,0:T(8,128)(2,1)}, bf16[4,72,128]{2,1,0:T(8,128)(2,1)S(1)}, u32[]{:S(2)}, u32[]{:S(2)}) collective-permute-start(bf16[4,72,128]{2,1,0:T(8,128)(2,1)} %get-tuple-element.32), channel_id=1, source_target_pairs={{0,12},{1,13},{2,14},{3,15},{4,24},{5,25},{6,26},{7,27},{8,20},{9,... | collective-permute-start | bytes 221192 | tf_op jit(solution)/shard_map/ppermute | solution.py:57
  119.1 4.3 %collective-permute-done.23 = bf16[4,72,128]{2,1,0:T(8,128)(2,1)S(1)} collective-permute-done((bf16[4,72,128]{2,1,0:T(8,128)(2,1)}, bf16[4,72,128]{2,1,0:T(8,128)(2,1)S(1)}, u32[]{:S(2)}, u32[]{:S(2)}) %collective-permute-start.23) | collective-permute-done | bytes 73760 | tf_op jit(solution)/shard_map/ppermute | solution.py:57
  125.7 2.7 %collective-permute-done.24 = bf16[2,72,128]{2,1,0:T(8,128)(2,1)S(1)} collective-permute-done((bf16[2,72,128]{2,1,0:T(8,128)(2,1)S(1)}, bf16[2,72,128]{2,1,0:T(8,128)(2,1)S(1)}, u32[]{:S(2)}, u32[]{:S(2)}) %collective-permute-start.24) | collective-permute-done | bytes 36896 | tf_op jit(solution)/shard_map/ppermute | solution.py:57
  128.6 2.6 %collective-permute-done.25 = bf16[1,72,128]{2,1,0:T(8,128)(2,1)S(1)} collective-permute-done((bf16[1,72,128]{2,1,0:T(8,128)(2,1)S(1)}, bf16[1,72,128]{2,1,0:T(8,128)(2,1)S(1)}, u32[]{:S(2)}, u32[]{:S(2)}) %collective-permute-start.25) | collective-permute-done | bytes 18464 | tf_op jit(solution)/shard_map/ppermute | solution.py:57
  131.8 15.3 %collective-permute-start.26 = (bf16[72,128]{1,0:T(8,128)(2,1)S(1)}, bf16[72,128]{1,0:T(8,128)(2,1)S(1)}, u32[]{:S(2)}, u32[]{:S(2)}) collective-permute-start(bf16[72,128]{1,0:T(8,128)(2,1)S(1)} %get-tuple-element.35), channel_id=1, source_target_pairs={{0,128},{128,0},{1,129},{129,1},{2,130},{130,2},{3,131},{131,3},{4... | collective-permute-start | bytes 55304 | tf_op jit(solution)/shard_map/ppermute | solution.py:596
  147.2 2.1 %order_posterior.1 = bf16[1,256,512]{2,1,0:T(8,128)(2,1)} custom-call(bf16[256,256]{1,0:T(8,128)(2,1)} %get-tuple-element.21.left_ref, bf16[256,256]{1,0:T(8,128)(2,1)} %get-tuple-element.22.right_ref.post_ref), custom_call_target="tpu_custom_call" | custom-call | tf_op jit(solution)/shard_map/order_posterior/pallas_call | solution.py:314
  (96 shorter events, 33.7 us)
Async XLA Ops:
  2.2 3.8 %collective-permute-start = (bf16[1,72,128]{2,1,0:T(8,128)(2,1)}, bf16[1,72,128]{2,1,0:T(8,128)(2,1)S(1)}, u32[]{:S(2)}, u32[]{:S(2)}) collective-permute-start(bf16[1,72,128]{2,1,0:T(8,128)(2,1)} %bitcast.27), channel_id=1, source_target_pairs={{0,4},{1,5},{2,6},{3,7},{4,0},{5,1},{6,2},{7,3},{8,12},{9,13},{10,... | collective-permute-start | bytes 55304 | tf_op jit(solution)/shard_map/ppermute | solution.py:57
  6.7 6.7 %collective-permute-start.1 = (bf16[2,72,128]{2,1,0:T(8,128)(2,1)S(1)}, bf16[2,72,128]{2,1,0:T(8,128)(2,1)S(1)}, u32[]{:S(2)}, u32[]{:S(2)}) collective-permute-start(bf16[2,72,128]{2,1,0:T(8,128)(2,1)S(1)} %pad_maximum_fusion.3), channel_id=1, source_target_pairs={{0,28},{1,29},{2,30},{3,31},{4,8},{5,9},{6,10},{7,11},{8,4},{9,5},... | collective-permute-start | bytes 110600 | tf_op jit(solution)/shard_map/ppermute | solution.py:57
  14.2 5.9 %collective-permute-start.2 = (bf16[4,72,128]{2,1,0:T(8,128)(2,1)S(1)}, bf16[4,72,128]{2,1,0:T(8,128)(2,1)S(1)}, u32[]{:S(2)}, u32[]{:S(2)}) collective-permute-start(bf16[4,72,128]{2,1,0:T(8,128)(2,1)S(1)} %pad_maximum_fusion.2.own_ref), channel_id=1, source_target_pairs={{0,12},{1,13},{2,14},{3,15},{4,24},{5,25},{6,26},{7,27},{8,20},{9,... | collective-permute-start | bytes 221192 | tf_op jit(solution)/shard_map/ppermute | solution.py:57
  22.3 8.1 %collective-permute-start.3 = (bf16[1,264,128]{2,1,0:T(8,128)(2,1)}, bf16[1,264,128]{2,1,0:T(8,128)(2,1)S(1)}, u32[]{:S(2)}, u32[]{:S(2)}) collective-permute-start(bf16[1,264,128]{2,1,0:T(8,128)(2,1)} %get-tuple-element.19), channel_id=1, source_target_pairs={{0,64},{1,65},{2,66},{3,67},{4,68},{5,69},{6,70},{7,71},{8,72},{9,... | collective-permute-start | bytes 202760 | tf_op jit(solution)/shard_map/ppermute | solution.py:49
  27.8 5.5 %collective-permute-start.9 = (bf16[2,264,128]{2,1,0:T(8,128)(2,1)S(1)}, bf16[2,264,128]{2,1,0:T(8,128)(2,1)S(1)}, u32[]{:S(2)}, u32[]{:S(2)}) collective-permute-start(bf16[2,264,128]{2,1,0:T(8,128)(2,1)S(1)} %pad_maximum_fusion.1), channel_id=1, source_target_pairs={{0,3},{1,2},{2,1},{3,0},{4,7},{5,6},{6,5},{7,4},{8,11},{9,10},{10,... | collective-permute-start | bytes 405512 | tf_op jit(solution)/shard_map/ppermute | solution.py:49
  31.3 5.7 %collective-permute-start.4 = (bf16[2,264,128]{2,1,0:T(8,128)(2,1)S(1)}, bf16[2,264,128]{2,1,0:T(8,128)(2,1)S(1)}, u32[]{:S(2)}, u32[]{:S(2)}) collective-permute-start(bf16[2,264,128]{2,1,0:T(8,128)(2,1)S(1)} %pad_maximum_fusion), channel_id=1, source_target_pairs={{0,96},{1,97},{2,98},{3,99},{4,100},{5,101},{6,102},{7,103},{8,104... | collective-permute-start | bytes 405512 | tf_op jit(solution)/shard_map/ppermute | solution.py:49
  33.4 6.9 %collective-permute-start.12 = (bf16[4,264,128]{2,1,0:T(8,128)(2,1)S(1)}, bf16[4,264,128]{2,1,0:T(8,128)(2,1)S(1)}, u32[]{:S(2)}, u32[]{:S(2)}) collective-permute-start(bf16[4,264,128]{2,1,0:T(8,128)(2,1)S(1)} %constant_dynamic-update-slice_fusion.3.b0), channel_id=1, source_target_pairs={{0,32},{1,33},{2,34},{3,35},{4,36},{5,37},{6,38},{7,39},{8,40},{9,... | collective-permute-start | bytes 811016 | tf_op jit(solution)/shard_map/ppermute | solution.py:49
  36.4 19.8 %collective-permute-start.11 = (bf16[4,264,128]{2,1,0:T(8,128)(2,1)S(1)}, bf16[4,264,128]{2,1,0:T(8,128)(2,1)S(1)}, u32[]{:S(2)}, u32[]{:S(2)}) collective-permute-start(bf16[4,264,128]{2,1,0:T(8,128)(2,1)S(1)} %constant_dynamic-update-slice_fusion.3.b0), channel_id=1, source_target_pairs={{0,96},{1,97},{2,98},{3,99},{4,100},{5,101},{6,102},{7,103},{8,104... | collective-permute-start | bytes 811016 | tf_op jit(solution)/shard_map/ppermute | solution.py:49
  37.0 19.2 %collective-permute-start.10 = (bf16[4,264,128]{2,1,0:T(8,128)(2,1)S(1)}, bf16[4,264,128]{2,1,0:T(8,128)(2,1)S(1)}, u32[]{:S(2)}, u32[]{:S(2)}) collective-permute-start(bf16[4,264,128]{2,1,0:T(8,128)(2,1)S(1)} %constant_dynamic-update-slice_fusion.3.b0), channel_id=1, source_target_pairs={{0,64},{1,65},{2,66},{3,67},{4,68},{5,69},{6,70},{7,71},{8,72},{9,... | collective-permute-start | bytes 811016 | tf_op jit(solution)/shard_map/ppermute | solution.py:49
  37.1 19.2 %collective-permute-start.7 = (bf16[4,264,128]{2,1,0:T(8,128)(2,1)S(1)}, bf16[4,264,128]{2,1,0:T(8,128)(2,1)S(1)}, u32[]{:S(2)}, u32[]{:S(2)}) collective-permute-start(bf16[4,264,128]{2,1,0:T(8,128)(2,1)S(1)} %constant_dynamic-update-slice_fusion.a0), channel_id=1, source_target_pairs={{0,2},{1,3},{2,0},{3,1},{4,6},{5,7},{6,4},{7,5},{8,10},{9,11},{10,... | collective-permute-start | bytes 811016 | tf_op jit(solution)/shard_map/ppermute | solution.py:49
  38.3 18.0 %collective-permute-start.6 = (bf16[4,264,128]{2,1,0:T(8,128)(2,1)S(1)}, bf16[4,264,128]{2,1,0:T(8,128)(2,1)S(1)}, u32[]{:S(2)}, u32[]{:S(2)}) collective-permute-start(bf16[4,264,128]{2,1,0:T(8,128)(2,1)S(1)} %constant_dynamic-update-slice_fusion.a0), channel_id=1, source_target_pairs={{0,3},{1,2},{2,1},{3,0},{4,7},{5,6},{6,5},{7,4},{8,11},{9,10},{10,... | collective-permute-start | bytes 811016 | tf_op jit(solution)/shard_map/ppermute | solution.py:49
  40.3 16.0 %collective-permute-start.5 = (bf16[4,264,128]{2,1,0:T(8,128)(2,1)S(1)}, bf16[4,264,128]{2,1,0:T(8,128)(2,1)S(1)}, u32[]{:S(2)}, u32[]{:S(2)}) collective-permute-start(bf16[4,264,128]{2,1,0:T(8,128)(2,1)S(1)} %constant_dynamic-update-slice_fusion.a0), channel_id=1, source_target_pairs={{0,1},{1,0},{2,3},{3,2},{4,5},{5,4},{6,7},{7,6},{8,9},{9,8},{10,11... | collective-permute-start | bytes 811016 | tf_op jit(solution)/shard_map/ppermute | solution.py:49
  81.2 16.6 %collective-permute-start.13 = (bf16[4,264,128]{2,1,0:T(8,128)(2,1)}, bf16[4,264,128]{2,1,0:T(8,128)(2,1)S(1)}, u32[]{:S(2)}, u32[]{:S(2)}) collective-permute-start(bf16[4,264,128]{2,1,0:T(8,128)(2,1)} %get-tuple-element.24), channel_id=1, source_target_pairs={{0,1},{1,0},{2,3},{3,2},{4,5},{5,4},{6,7},{7,6},{8,9},{9,8},{10,11... | collective-permute-start | bytes 811016 | tf_op jit(solution)/shard_map/ppermute | solution.py:49
  82.7 15.1 %collective-permute-start.14 = (bf16[4,264,128]{2,1,0:T(8,128)(2,1)}, bf16[4,264,128]{2,1,0:T(8,128)(2,1)S(1)}, u32[]{:S(2)}, u32[]{:S(2)}) collective-permute-start(bf16[4,264,128]{2,1,0:T(8,128)(2,1)} %get-tuple-element.25), channel_id=1, source_target_pairs={{0,3},{1,2},{2,1},{3,0},{4,7},{5,6},{6,5},{7,4},{8,11},{9,10},{10,... | collective-permute-start | bytes 811016 | tf_op jit(solution)/shard_map/ppermute | solution.py:49
  85.0 12.9 %collective-permute-start.15 = (bf16[4,264,128]{2,1,0:T(8,128)(2,1)}, bf16[4,264,128]{2,1,0:T(8,128)(2,1)S(1)}, u32[]{:S(2)}, u32[]{:S(2)}) collective-permute-start(bf16[4,264,128]{2,1,0:T(8,128)(2,1)} %get-tuple-element.26), channel_id=1, source_target_pairs={{0,2},{1,3},{2,0},{3,1},{4,6},{5,7},{6,4},{7,5},{8,10},{9,11},{10,... | collective-permute-start | bytes 811016 | tf_op jit(solution)/shard_map/ppermute | solution.py:49
  94.4 5.9 %collective-permute-start.18 = (bf16[4,264,128]{2,1,0:T(8,128)(2,1)}, bf16[4,264,128]{2,1,0:T(8,128)(2,1)S(1)}, u32[]{:S(2)}, u32[]{:S(2)}) collective-permute-start(bf16[4,264,128]{2,1,0:T(8,128)(2,1)} %get-tuple-element.28), channel_id=1, source_target_pairs={{0,64},{1,65},{2,66},{3,67},{4,68},{5,69},{6,70},{7,71},{8,72},{9,... | collective-permute-start | bytes 811016 | tf_op jit(solution)/shard_map/ppermute | solution.py:49
  95.3 9.2 %collective-permute-start.19 = (bf16[4,264,128]{2,1,0:T(8,128)(2,1)}, bf16[4,264,128]{2,1,0:T(8,128)(2,1)S(1)}, u32[]{:S(2)}, u32[]{:S(2)}) collective-permute-start(bf16[4,264,128]{2,1,0:T(8,128)(2,1)} %get-tuple-element.29), channel_id=1, source_target_pairs={{0,96},{1,97},{2,98},{3,99},{4,100},{5,101},{6,102},{7,103},{8,104... | collective-permute-start | bytes 811016 | tf_op jit(solution)/shard_map/ppermute | solution.py:49
  97.8 7.1 %collective-permute-start.20 = (bf16[4,264,128]{2,1,0:T(8,128)(2,1)}, bf16[4,264,128]{2,1,0:T(8,128)(2,1)S(1)}, u32[]{:S(2)}, u32[]{:S(2)}) collective-permute-start(bf16[4,264,128]{2,1,0:T(8,128)(2,1)} %get-tuple-element.30), channel_id=1, source_target_pairs={{0,32},{1,33},{2,34},{3,35},{4,36},{5,37},{6,38},{7,39},{8,40},{9,... | collective-permute-start | bytes 811016 | tf_op jit(solution)/shard_map/ppermute | solution.py:49
  98.0 9.9 %collective-permute-start.16 = (bf16[2,264,128]{2,1,0:T(8,128)(2,1)S(1)}, bf16[2,264,128]{2,1,0:T(8,128)(2,1)S(1)}, u32[]{:S(2)}, u32[]{:S(2)}) collective-permute-start(bf16[2,264,128]{2,1,0:T(8,128)(2,1)S(1)} %slice.69), channel_id=1, source_target_pairs={{0,96},{1,97},{2,98},{3,99},{4,100},{5,101},{6,102},{7,103},{8,104... | collective-permute-start | bytes 405512 | tf_op jit(solution)/shard_map/ppermute | solution.py:49
  106.1 5.4 %collective-permute-start.21 = (bf16[2,264,128]{2,1,0:T(8,128)(2,1)S(1)}, bf16[2,264,128]{2,1,0:T(8,128)(2,1)S(1)}, u32[]{:S(2)}, u32[]{:S(2)}) collective-permute-start(bf16[2,264,128]{2,1,0:T(8,128)(2,1)S(1)} %slice.68), channel_id=1, source_target_pairs={{0,3},{1,2},{2,1},{3,0},{4,7},{5,6},{6,5},{7,4},{8,11},{9,10},{10,... | collective-permute-start | bytes 405512 | tf_op jit(solution)/shard_map/ppermute | solution.py:49
  108.0 4.2 %collective-permute-start.17 = (bf16[1,264,128]{2,1,0:T(8,128)(2,1)S(1)}, bf16[1,264,128]{2,1,0:T(8,128)(2,1)S(1)}, u32[]{:S(2)}, u32[]{:S(2)}) collective-permute-start(bf16[1,264,128]{2,1,0:T(8,128)(2,1)S(1)} %slice.71), channel_id=1, source_target_pairs={{0,64},{1,65},{2,66},{3,67},{4,68},{5,69},{6,70},{7,71},{8,72},{9,... | collective-permute-start | bytes 202760 | tf_op jit(solution)/shard_map/ppermute | solution.py:49
  117.4 6.0 %collective-permute-start.23 = (bf16[4,72,128]{2,1,0:T(8,128)(2,1)}, bf16[4,72,128]{2,1,0:T(8,128)(2,1)S(1)}, u32[]{:S(2)}, u32[]{:S(2)}) collective-permute-start(bf16[4,72,128]{2,1,0:T(8,128)(2,1)} %get-tuple-element.32), channel_id=1, source_target_pairs={{0,12},{1,13},{2,14},{3,15},{4,24},{5,25},{6,26},{7,27},{8,20},{9,... | collective-permute-start | bytes 221192 | tf_op jit(solution)/shard_map/ppermute | solution.py:57
  124.4 4.1 %collective-permute-start.24 = (bf16[2,72,128]{2,1,0:T(8,128)(2,1)S(1)}, bf16[2,72,128]{2,1,0:T(8,128)(2,1)S(1)}, u32[]{:S(2)}, u32[]{:S(2)}) collective-permute-start(bf16[2,72,128]{2,1,0:T(8,128)(2,1)S(1)} %slice.72), channel_id=1, source_target_pairs={{0,28},{1,29},{2,30},{3,31},{4,8},{5,9},{6,10},{7,11},{8,4},{9,5},... | collective-permute-start | bytes 110600 | tf_op jit(solution)/shard_map/ppermute | solution.py:57
  131.8 17.4 %collective-permute-start.26 = (bf16[72,128]{1,0:T(8,128)(2,1)S(1)}, bf16[72,128]{1,0:T(8,128)(2,1)S(1)}, u32[]{:S(2)}, u32[]{:S(2)}) collective-permute-start(bf16[72,128]{1,0:T(8,128)(2,1)S(1)} %get-tuple-element.35), channel_id=1, source_target_pairs={{0,128},{128,0},{1,129},{129,1},{2,130},{130,2},{3,131},{131,3},{4... | collective-permute-start | bytes 55304 | tf_op jit(solution)/shard_map/ppermute | solution.py:596
  (19 other events, 107.9 us)

commit v2 on v1

--- a/solution.py
+++ b/solution.py
@@ -21,7 +21,7 @@
 CHUNK = 640
 STEPS = FC // CHUNK
 PART = 1664
-ROWS = 264
+ROWS = 40
 NX, NY, NZ = 4, 4, 8
 GRAY = (0, 1, 3, 2)
 Z_ORDER = (0, -1, 1, 2, -3, -2, -4, -5)
@@ -105,25 +105,25 @@
 def pack_kernel(p_ref, out_ref):
     lane = iota((8, LANE), 1)
     sub = iota((8, LANE), 0)
-    tails = []
     for color in range(2):
+        base = color * ROWS
         extra = jnp.zeros((8, LANE), jnp.float32)
         for kl in range(2):
             for c in range(2):
                 rows = p_ref[0, color * 2 + kl, :, c, :].astype(jnp.float32)
                 group = kl * 2 + c
-                start = color * 32 + group * 8
-                out_ref[start : start + 8, :] = rows[:, :LANE].astype(jnp.bfloat16)
+                start = base + group * 8
+                out_ref[0, start : start + 8, :] = rows[:, :LANE].astype(jnp.bfloat16)
                 first = 2 * (group * 8 + sub)
                 extra += jnp.where(lane == first, rows[:, LANE : LANE + 1], 0.0)
                 extra += jnp.where(lane == first + 1, rows[:, LANE + 1 : LANE + 2], 0.0)
-        tails.append(jnp.sum(extra, axis=0, keepdims=True))
-    both = jnp.where(sub == 0, tails[0], tails[1])
-    out_ref[64:72, :] = both.astype(jnp.bfloat16)
+        row = jnp.sum(extra, axis=0, keepdims=True)
+        tail = jnp.broadcast_to(row, (8, LANE))
+        out_ref[0, base + 32 : base + 40, :] = tail.astype(jnp.bfloat16)
 
 
 def pack_sections(projections):
-    shape = jax.ShapeDtypeStruct((72, LANE), jnp.bfloat16)
+    shape = jax.ShapeDtypeStruct((1, 2 * ROWS, LANE), jnp.bfloat16)
     return pl.pallas_call(pack_kernel, out_shape=shape, name="pack_sections")(projections)
 
 
@@ -186,15 +186,14 @@
             def body(far, carry, ref=ref, near=near, color=color):
                 cls, chunks = sources(pos_ref, near, far, color)
                 rows = pl.ds(pl.multiple_of(cls * 64 + color * 32, 32), 32)
-                tails = ref[far, 256:264].astype(jnp.float32)
                 for slot, j in enumerate(chunks):
-                    piece = ref[far, slot * 32 : slot * 32 + 32].astype(jnp.float32)
-                    turned = pltpu.roll(piece, 2 * j, 1)
+                    piece = ref[far, slot].astype(jnp.float32)
+                    turned = pltpu.roll(piece[:32], 2 * j, 1)
                     here = pl.ds(pl.multiple_of(j * LANE, LANE), LANE)
                     after = pl.ds(pl.multiple_of((j + 1) * LANE, LANE), LANE)
                     pltpu.store(nat_ref.at[rows, here], turned, mask=lane >= 2 * j)
                     pltpu.store(nat_ref.at[rows, after], turned, mask=lane < 2 * j)
-                    ex_ref[pl.ds(cls * 128 + color * 64 + j, 1), :] = tails[slot : slot + 1]
+                    ex_ref[pl.ds(cls * 128 + color * 64 + j, 1), :] = piece[32:33]
                 return carry
 
             lax.fori_loop(0, 4, body, 0)
@@ -215,8 +214,8 @@
 
 
 def score_kernel(
-    pos_ref, a0, a1, a2, a3, b0, b1, b2, b3, w_hbm, table_ref, inv_ref,
-    cos_ref, sin_ref, group_ref, orient_ref, left_ref, right_ref, p0, p1, p2, p3,
+    pos_ref, a0, a1, a2, a3, b0, b1, b2, b3, w_hbm, table_ref, inv_ref, cos_ref, sin_ref,
+    group_ref, orient_ref, left_ref, right_ref, p0, p1, p2, p3,
     nat_ref, ex_ref, shift_ref, acc_ref, norm_ref, w_ref, sem_ref, slab_ref, sum_ref,
 ):
     for step in range(STEPS):
@@ -344,7 +343,7 @@
             jax.ShapeDtypeStruct((wide // 2, NP), jnp.bfloat16),
             jax.ShapeDtypeStruct((wide // 2, NP), jnp.bfloat16),
         ]
-        + [jax.ShapeDtypeStruct((4, ROWS, LANE), jnp.bfloat16)] * 4,
+        + [jax.ShapeDtypeStruct((4, NZ, ROWS, LANE), jnp.bfloat16)] * 4,
         compiler_params=pltpu.CompilerParams(vmem_limit_bytes=VMEM_LIMIT),
         name="score",
     )(pos, *a, *b, weighted, table, inverse, cosine, sine, group_row, orient)
@@ -407,15 +406,14 @@
         def pack(far, carry, near=near, out=out):
             cls, chunks = sources(pos_ref, near, far, color)
             rows = pl.ds(pl.multiple_of(cls * 32, 32), 32)
-            tails = []
             for slot, j in enumerate(chunks):
                 here = pl.ds(pl.multiple_of(j * LANE, LANE), LANE)
                 after = pl.ds(pl.multiple_of((j + 1) * LANE, LANE), LANE)
                 both = jnp.where(lane >= 2 * j, slab_ref[rows, here], slab_ref[rows, after])
                 main = pltpu.roll(both, LANE - 2 * j, 1)
-                tails.append(ex_ref[pl.ds(cls * 64 + j, 1), :])
-                out[far, slot * 32 : slot * 32 + 32, :] = main.astype(jnp.bfloat16)
-            out[far, 256:264, :] = jnp.concatenate(tails, axis=0).astype(jnp.bfloat16)
+                tail = ex_ref[pl.ds(cls * 64 + j, 1), :]
+                out[far, slot, 0:32, :] = main.astype(jnp.bfloat16)
+                out[far, slot, 32:40, :] = jnp.broadcast_to(tail, (8, LANE)).astype(jnp.bfloat16)
             return carry
 
         lax.fori_loop(0, 4, pack, 0)
@@ -440,7 +438,7 @@
 def project_back(pos, post, weighted, cosine, sine):
     return pl.pallas_call(
         back_kernel,
-        in_specs=[SMEM, VMEM, ANY] + [VMEM] * 2,
+        in_specs=[SMEM, VMEM, ANY, VMEM, VMEM],
         out_specs=[VMEM] * 4,
         scratch_shapes=[
             pltpu.VMEM((64, FC), jnp.float32),
@@ -449,7 +447,7 @@
             pltpu.VMEM((STEPS, NP, 2 * CHUNK), jnp.bfloat16),
             pltpu.SemaphoreType.DMA((STEPS,)),
         ],
-        out_shape=[jax.ShapeDtypeStruct((4, ROWS, LANE), jnp.bfloat16)] * 4,
+        out_shape=[jax.ShapeDtypeStruct((4, NZ, ROWS, LANE), jnp.bfloat16)] * 4,
         compiler_params=pltpu.CompilerParams(vmem_limit_bytes=VMEM_LIMIT),
         name="project_back",
     )(pos, post, weighted, cosine, sine)
@@ -467,9 +465,9 @@
         return jnp.concatenate([one, two], axis=1)
 
     for color in range(2):
-        base = color * 32
-        own_row = own_ref[64 + color : 65 + color, :]
-        partner_row = partner_ref[64:72, :].astype(jnp.float32)[color : color + 1]
+        base = color * ROWS
+        own_row = own_ref[base + 32 : base + 33, :]
+        partner_row = partner_ref[base + 32 : base + 40, :].astype(jnp.float32)[0:1]
         for kl in range(2):
             k = color * 2 + kl
             main, edge = 0.0, 0.0
@@ -497,53 +495,6 @@
     )(own, partner)
 
 
-def regroup_kernel(own_ref, got_ref, left_ref, right_ref):
-    tails = ([], [])
-    for slot in range(NZ):
-        ref = own_ref if slot < 4 else got_ref
-        last = ref[slot % 4, 64:72, :].astype(jnp.float32)
-        for color, out in ((0, left_ref), (1, right_ref)):
-            out[0, slot * 32 : slot * 32 + 32, :] = ref[slot % 4, color * 32 : color * 32 + 32, :]
-            tails[color].append(last[color : color + 1])
-    left_ref[0, 256:264, :] = jnp.concatenate(tails[0], axis=0).astype(jnp.bfloat16)
-    right_ref[0, 256:264, :] = jnp.concatenate(tails[1], axis=0).astype(jnp.bfloat16)
-
-
-def regroup(own, got):
-    shape = jax.ShapeDtypeStruct((1, ROWS, LANE), jnp.bfloat16)
-    return pl.pallas_call(regroup_kernel, out_shape=(shape, shape), name="regroup")(own, got)
-
-
-def ungroup_kernel(l0_ref, l1_ref, r0_ref, r1_ref, keep_ref, send_ref):
-    sub = iota((8, LANE), 0)
-    tails = []
-    for first, second in ((l0_ref, l1_ref), (r0_ref, r1_ref)):
-        tails.append(first[0, 256:264, :] + second[0, 256:264, :].astype(jnp.float32))
-    for slot in range(NZ):
-        parts = []
-        rows = slice(slot * 32, slot * 32 + 32)
-        for first, second in ((l0_ref, l1_ref), (r0_ref, r1_ref)):
-            parts.append(first[0, rows, :] + second[0, rows, :].astype(jnp.float32))
-        left, right = tails[0][slot : slot + 1], tails[1][slot : slot + 1]
-        parts.append(jnp.where(sub == 0, left, jnp.where(sub == 1, right, 0.0)))
-        value = jnp.concatenate(parts, axis=0)
-        if slot < 4:
-            keep_ref[slot] = value
-        else:
-            send_ref[slot - 4] = value.astype(jnp.bfloat16)
-
-
-def ungroup(l0, l1, r0, r1):
-    return pl.pallas_call(
-        ungroup_kernel,
-        out_shape=(
-            jax.ShapeDtypeStruct((4, 72, LANE), jnp.float32),
-            jax.ShapeDtypeStruct((4, 72, LANE), jnp.bfloat16),
-        ),
-        name="ungroup",
-    )(l0, l1, r0, r1)
-
-
 def added(parts):
     total = parts[0].astype(jnp.float32)
     for part in parts[1:]:
@@ -559,11 +510,10 @@
     cosine, sine = phases(trans_ids[0], FC)
     weighted = weight_images(images, ctf_table, ctf_group)
 
-    along = pack_sections(projections)[None]
-    for odd in (-1, 1):
+    along = pack_sections(projections)
+    for odd in (-1, 1, -3):
         along = jnp.concatenate([along, trade_z(along, odd)])
-    got = trade_z(along, -3)
-    left, right = regroup(along, got)
+    left, right = along[None, :, :ROWS], along[None, :, ROWS:]
     for mask in (1, 3):
         left = jnp.concatenate([left, trade(left, my=mask)])
         right = jnp.concatenate([right, trade(right, mx=mask)])
@@ -584,14 +534,14 @@
         parts.append(trade(pieces[d], my=GRAY[d]))
     right = added(parts)
     posterior = order_posterior(post_left, post_right)
-    left = added([left[:2], trade(left[2:].astype(jnp.bfloat16), my=3)])
-    right = added([right[:2], trade(right[2:].astype(jnp.bfloat16), mx=3)])
-    left_got = trade(left[1:].astype(jnp.bfloat16), my=1)
-    right_got = trade(right[1:].astype(jnp.bfloat16), mx=1)
-    own, sent = ungroup(left, left_got, right, right_got)
-    own = own + trade_z(sent, -3).astype(jnp.float32)
-    for odd, size in ((1, 2), (-1, 1)):
-        own = added([own[:size], trade_z(own[size:].astype(jnp.bfloat16), odd)])
+    for mask, size in ((3, 2), (1, 1)):
+        left, right = left.astype(jnp.bfloat16), right.astype(jnp.bfloat16)
+        left = added([left[:size], trade(left[size:], my=mask)])
+        right = added([right[:size], trade(right[size:], mx=mask)])
+    own = jnp.concatenate([left[0], right[0]], axis=1)
+    for odd, size in ((-3, 4), (1, 2), (-1, 1)):
+        own = own.astype(jnp.bfloat16)
+        own = added([own[:size], trade_z(own[size:], odd)])
     own = own[0]
     partner = lax.ppermute(own.astype(jnp.bfloat16), "half", [(0, 1), (1, 0)])
     slab, product = finish(own, partner)

time: 152 us -> 150 us (0.987)
  starting transfers between devices: 52.5 us -> 56.6 us
  Pallas kernels: 54.5 us -> 51.4 us
  local copies, waits for them, and re-layouts: 3.94 us -> 1.83 us
  other arithmetic: 9.21 us -> 7.66 us
    pallas_call x3 -> x1, Pallas kernels: 12.7 us -> 9.41 us  [project_back(): pl.pallas_call(back_kernel, in_specs=[SMEM, VMEM, ANY, VMEM, VMEM], out_s...]
    ppermute x20, starting transfers between devices: 24.4 us -> 27.6 us  [trade(): return lax.ppermute(value, PAIR, pairs)]
    add x6 -> x0, other arithmetic: 2.21 us -> none  [the longest x5 1.29 us: added(): total = total + part.astype(jnp.float32)]
    unnamed x35 -> x20, local copies, waits for them, and re-layouts: 3.82 us -> 1.75 us
  transfers between devices with their start and end apart: 27 -> 27, of which waited for: 14 -> 14; matrix products, arithmetic and copies ran while one was open for 5% -> 3% of each run, Pallas kernels for 16% -> 16%
where the time goes in v2:
time: 150 us
  starting transfers between devices  56.6 us (38%)
  Pallas kernels  51.4 us (34%)
  waiting for transfers between devices  30.6 us (20%)
  other arithmetic  7.66 us (5%)
  local copies, waits for them, and re-layouts  1.83 us (1%)
  between operations  1.58 us (1%)
    ppermute x20, starting transfers between devices, trade(): return lax.ppermute(value, PAIR, pairs)  27.6 us
    pallas_call x1, Pallas kernels, score(): pl.pallas_call(score_kernel, in_specs=[SMEM] + [VMEM] * 8 + [ANY] + [VMEM...  24.1 us
    ppermute x6, waiting for transfers between devices, trade_z(): return lax.ppermute(value, PAIR, pairs)  17.1 us
    ppermute x1, starting transfers between devices, run(): partner = lax.ppermute(own.astype(jnp.bfloat16), 'half', [(0, 1), (1, 0)])  16.6 us
    ppermute x20, waiting for transfers between devices, trade(): return lax.ppermute(value, PAIR, pairs)  13.5 us
    pallas_call x1, Pallas kernels, weight_images(): pl.pallas_call(weight_kernel, grid=(FC // PART,), in_specs=[pl.BlockSpec(...  12.8 us
    ppermute x6, starting transfers between devices, trade_z(): return lax.ppermute(value, PAIR, pairs)  12.4 us
    pallas_call x1, Pallas kernels, project_back(): pl.pallas_call(back_kernel, in_specs=[SMEM, VMEM, ANY, VMEM, VMEM], out_s...  9.41 us
  transfers between devices with their start and end apart: 27, of which 14 were waited for; matrix products, arithmetic and copies ran while one was open for 3% of the time, Pallas kernels for 16%

profile of v2, /device:TPU:1, one launch (start us, length us, event | category | flops | bytes accessed | tf_op | source)
XLA Modules:
  0.0 149.7 jit_solution(3541127598915700515)
XLA Ops:
  2.2 2.5 %collective-permute-start = (bf16[1,80,128]{2,1,0:T(8,128)(2,1)}, bf16[1,80,128]{2,1,0:T(8,128)(2,1)S(1)}, u32[]{:S(2)}, u32[]{:S(2)}) collective-permute-start(bf16[1,80,128]{2,1,0:T(8,128)(2,1)} %pack_sections.1), channel_id=1, source_target_pairs={{0,4},{1,5},{2,6},{3,7},{4,0},{5,1},{6,2},{7,3},{8,12},{9,13},{10,... | collective-permute-start | bytes 61448 | tf_op jit(solution)/shard_map/ppermute | solution.py:57
  6.7 5.4 %collective-permute-start.1 = (bf16[2,80,128]{2,1,0:T(8,128)(2,1)S(1)}, bf16[2,80,128]{2,1,0:T(8,128)(2,1)S(1)}, u32[]{:S(2)}, u32[]{:S(2)}) collective-permute-start(bf16[2,80,128]{2,1,0:T(8,128)(2,1)S(1)} %pad_maximum_fusion.7), channel_id=1, source_target_pairs={{0,28},{1,29},{2,30},{3,31},{4,8},{5,9},{6,10},{7,11},{8,4},{9,5},... | collective-permute-start | bytes 122888 | tf_op jit(solution)/shard_map/ppermute | solution.py:57
  14.3 1.7 %collective-permute-start.2 = (bf16[4,80,128]{2,1,0:T(8,128)(2,1)S(1)}, bf16[4,80,128]{2,1,0:T(8,128)(2,1)S(1)}, u32[]{:S(2)}, u32[]{:S(2)}) collective-permute-start(bf16[4,80,128]{2,1,0:T(8,128)(2,1)S(1)} %pad_maximum_fusion.6), channel_id=1, source_target_pairs={{0,12},{1,13},{2,14},{3,15},{4,24},{5,25},{6,26},{7,27},{8,20},{9,... | collective-permute-start | bytes 245768 | tf_op jit(solution)/shard_map/ppermute | solution.py:57
  16.0 4.3 %collective-permute-done.2 = bf16[4,80,128]{2,1,0:T(8,128)(2,1)S(1)} collective-permute-done((bf16[4,80,128]{2,1,0:T(8,128)(2,1)S(1)}, bf16[4,80,128]{2,1,0:T(8,128)(2,1)S(1)}, u32[]{:S(2)}, u32[]{:S(2)}) %collective-permute-start.2) | collective-permute-done | bytes 81952 | tf_op jit(solution)/shard_map/ppermute | solution.py:57
  24.5 2.8 %collective-permute-start.4 = (bf16[2,8,40,128]{3,2,1,0:T(8,128)(2,1)S(1)}, bf16[2,8,40,128]{3,2,1,0:T(8,128)(2,1)S(1)}, u32[]{:S(2)}, u32[]{:S(2)}) collective-permute-start(bf16[2,8,40,128]{3,2,1,0:T(8,128)(2,1)S(1)} %pad_maximum_fusion.3), channel_id=1, source_target_pairs={{0,96},{1,97},{2,98},{3,99},{4,100},{5,101},{6,102},{7,103},{8,104... | collective-permute-start | bytes 491528 | tf_op jit(solution)/shard_map/ppermute | solution.py:49
  27.4 2.6 %collective-permute-start.9 = (bf16[2,8,40,128]{3,2,1,0:T(8,128)(2,1)S(1)}, bf16[2,8,40,128]{3,2,1,0:T(8,128)(2,1)S(1)}, u32[]{:S(2)}, u32[]{:S(2)}) collective-permute-start(bf16[2,8,40,128]{3,2,1,0:T(8,128)(2,1)S(1)} %pad_maximum_fusion.4), channel_id=1, source_target_pairs={{0,3},{1,2},{2,1},{3,0},{4,7},{5,6},{6,5},{7,4},{8,11},{9,10},{10,... | collective-permute-start | bytes 491528 | tf_op jit(solution)/shard_map/ppermute | solution.py:49
  30.1 2.8 %collective-permute-start.7 = (bf16[4,8,40,128]{3,2,1,0:T(8,128)(2,1)S(1)}, bf16[4,8,40,128]{3,2,1,0:T(8,128)(2,1)S(1)}, u32[]{:S(2)}, u32[]{:S(2)}) collective-permute-start(bf16[4,8,40,128]{3,2,1,0:T(8,128)(2,1)S(1)} %pad_maximum_fusion.a0), channel_id=1, source_target_pairs={{0,2},{1,3},{2,0},{3,1},{4,6},{5,7},{6,4},{7,5},{8,10},{9,11},{10,... | collective-permute-start | bytes 983048 | tf_op jit(solution)/shard_map/ppermute | solution.py:49
  34.6 1.9 %collective-permute-start.12 = (bf16[4,8,40,128]{3,2,1,0:T(8,128)(2,1)S(1)}, bf16[4,8,40,128]{3,2,1,0:T(8,128)(2,1)S(1)}, u32[]{:S(2)}, u32[]{:S(2)}) collective-permute-start(bf16[4,8,40,128]{3,2,1,0:T(8,128)(2,1)S(1)} %pad_maximum_fusion.1.b0), channel_id=1, source_target_pairs={{0,32},{1,33},{2,34},{3,35},{4,36},{5,37},{6,38},{7,39},{8,40},{9,... | collective-permute-start | bytes 983048 | tf_op jit(solution)/shard_map/ppermute | solution.py:49
  38.2 1.8 %fusion = (f32[8,8320]{1,0:T(8,128)}, f32[8,8320]{1,0:T(8,128)}) fusion(f32[8320]{0:T(1024)S(1)} %get-tuple-element.35, f32[8]{0:T(128)S(1)} %get-tuple-element.34, f32[8320]{0:T(1024)S(1)} %get-tuple-element.36, f32[8]{0:T(128)S(1)} %get-tuple-element.33), kind=kLoop, calls=%fused_computation.7 | loop fusion | flops 266240 | bytes 599104 | tf_op jit(solution)/shard_map/sin | solution.py:84
  40.7 12.8 %weight_images.1.w_hbm = bf16[256,16640]{1,0:T(8,128)(2,1)} custom-call(bf16[1,256,2,8320]{3,2,1,0:T(2,128)(2,1)} %image_ref.1, f32[1,32,8320]{2,1,0:T(8,128)} %table_ref.3, s32[1,256]{1,0:T(1,128)} %group_ref.3), custom_call_target="tpu_custom_call" | custom-call | tf_op jit(solution)/shard_map/weight_images/pallas_call | solution.py:156
  55.4 24.1 %score.1 = (bf16[256,256]{1,0:T(8,128)(2,1)}, bf16[256,256]{1,0:T(8,128)(2,1)}, bf16[4,8,40,128]{3,2,1,0:T(8,128)(2,1)}, bf16[4,8,40,128]{3,2,1,0:T(8,128)(2,1)}...) custom-call(s32[4]{0:T(128)} %pad_add_fusion.pos_ref, bf16[4,8,40,128]{3,2,1,0:T(8,128)(2,1)} %copy-done, ...), custom_call_target="tpu_custom_call" | custom-call | tf_op jit(solution)/shard_map/score/pallas_call | solution.py:327
  81.0 1.8 %collective-permute-start.14 = (bf16[4,8,40,128]{3,2,1,0:T(8,128)(2,1)}, bf16[4,8,40,128]{3,2,1,0:T(8,128)(2,1)S(1)}, u32[]{:S(2)}, u32[]{:S(2)}) collective-permute-start(bf16[4,8,40,128]{3,2,1,0:T(8,128)(2,1)} %get-tuple-element.19), channel_id=1, source_target_pairs={{0,3},{1,2},{2,1},{3,0},{4,7},{5,6},{6,5},{7,4},{8,11},{9,10},{10,... | collective-permute-start | bytes 983048 | tf_op jit(solution)/shard_map/ppermute | solution.py:49
  83.0 9.4 %project_back.1 = (bf16[4,8,40,128]{3,2,1,0:T(8,128)(2,1)}, bf16[4,8,40,128]{3,2,1,0:T(8,128)(2,1)}, bf16[4,8,40,128]{3,2,1,0:T(8,128)(2,1)}, bf16[4,8,40,128]{3,2,1,0:T(8,128)(2,1)}) custom-call(s32[4]{0:T(128)} %pad_add_fusion.pos_ref, bf16[256,256]{1,0:T(8,128)(2,1)} %get-tuple-element.16.right_ref.post_ref, bf16[256,16640]{1,0:T(8,128)(2,1)} %weight_images.1.w_hbm, ...), custom_call_target="tpu_custom_call" | custom-call | tf_op jit(solution)/shard_map/project_back/pallas_call | solution.py:439
  93.7 2.7 %collective-permute-start.19 = (bf16[4,8,40,128]{3,2,1,0:T(8,128)(2,1)}, bf16[4,8,40,128]{3,2,1,0:T(8,128)(2,1)S(1)}, u32[]{:S(2)}, u32[]{:S(2)}) collective-permute-start(bf16[4,8,40,128]{3,2,1,0:T(8,128)(2,1)} %get-tuple-element.23), channel_id=1, source_target_pairs={{0,96},{1,97},{2,98},{3,99},{4,100},{5,101},{6,102},{7,103},{8,104... | collective-permute-start | bytes 983048 | tf_op jit(solution)/shard_map/ppermute | solution.py:49
  96.8 1.8 %collective-permute-start.16 = (bf16[2,8,40,128]{3,2,1,0:T(8,128)(2,1)S(1)}, bf16[2,8,40,128]{3,2,1,0:T(8,128)(2,1)S(1)}, u32[]{:S(2)}, u32[]{:S(2)}) collective-permute-start(bf16[2,8,40,128]{3,2,1,0:T(8,128)(2,1)S(1)} %slice.67), channel_id=1, source_target_pairs={{0,96},{1,97},{2,98},{3,99},{4,100},{5,101},{6,102},{7,103},{8,104... | collective-permute-start | bytes 491528 | tf_op jit(solution)/shard_map/ppermute | solution.py:49
  99.0 5.6 %collective-permute-done.19 = bf16[4,8,40,128]{3,2,1,0:T(8,128)(2,1)S(1)} collective-permute-done((bf16[4,8,40,128]{3,2,1,0:T(8,128)(2,1)}, bf16[4,8,40,128]{3,2,1,0:T(8,128)(2,1)S(1)}, u32[]{:S(2)}, u32[]{:S(2)}) %collective-permute-start.19) | collective-permute-done | bytes 327712 | tf_op jit(solution)/shard_map/ppermute | solution.py:49
  105.8 2.2 %collective-permute-start.21 = (bf16[2,8,40,128]{3,2,1,0:T(8,128)(2,1)S(1)}, bf16[2,8,40,128]{3,2,1,0:T(8,128)(2,1)S(1)}, u32[]{:S(2)}, u32[]{:S(2)}) collective-permute-start(bf16[2,8,40,128]{3,2,1,0:T(8,128)(2,1)S(1)} %slice.71), channel_id=1, source_target_pairs={{0,3},{1,2},{2,1},{3,0},{4,7},{5,6},{6,5},{7,4},{8,11},{9,10},{10,... | collective-permute-start | bytes 491528 | tf_op jit(solution)/shard_map/ppermute | solution.py:49
  108.7 2.8 %collective-permute-done.21 = bf16[2,8,40,128]{3,2,1,0:T(8,128)(2,1)S(1)} collective-permute-done((bf16[2,8,40,128]{3,2,1,0:T(8,128)(2,1)S(1)}, bf16[2,8,40,128]{3,2,1,0:T(8,128)(2,1)S(1)}, u32[]{:S(2)}, u32[]{:S(2)}) %collective-permute-start.21) | collective-permute-done | bytes 163872 | tf_op jit(solution)/shard_map/ppermute | solution.py:49
  112.6 2.7 %collective-permute-done.22 = bf16[1,8,40,128]{3,2,1,0:T(8,128)(2,1)S(1)} collective-permute-done((bf16[1,8,40,128]{3,2,1,0:T(8,128)(2,1)S(1)}, bf16[1,8,40,128]{3,2,1,0:T(8,128)(2,1)S(1)}, u32[]{:S(2)}, u32[]{:S(2)}) %collective-permute-start.22) | collective-permute-done | bytes 81952 | tf_op jit(solution)/shard_map/ppermute | solution.py:49
  117.0 4.4 %collective-permute-done.23 = bf16[4,80,128]{2,1,0:T(8,128)(2,1)S(1)} collective-permute-done((bf16[4,80,128]{2,1,0:T(8,128)(2,1)S(1)}, bf16[4,80,128]{2,1,0:T(8,128)(2,1)S(1)}, u32[]{:S(2)}, u32[]{:S(2)}) %collective-permute-start.23) | collective-permute-done | bytes 81952 | tf_op jit(solution)/shard_map/ppermute | solution.py:57
  122.5 3.1 %collective-permute-done.24 = bf16[2,80,128]{2,1,0:T(8,128)(2,1)S(1)} collective-permute-done((bf16[2,80,128]{2,1,0:T(8,128)(2,1)S(1)}, bf16[2,80,128]{2,1,0:T(8,128)(2,1)S(1)}, u32[]{:S(2)}, u32[]{:S(2)}) %collective-permute-start.24) | collective-permute-done | bytes 40992 | tf_op jit(solution)/shard_map/ppermute | solution.py:57
  125.7 2.6 %collective-permute-done.25 = bf16[1,80,128]{2,1,0:T(8,128)(2,1)S(1)} collective-permute-done((bf16[1,80,128]{2,1,0:T(8,128)(2,1)S(1)}, bf16[1,80,128]{2,1,0:T(8,128)(2,1)S(1)}, u32[]{:S(2)}, u32[]{:S(2)}) %collective-permute-start.25) | collective-permute-done | bytes 20512 | tf_op jit(solution)/shard_map/ppermute | solution.py:57
  128.9 16.6 %collective-permute-start.26 = (bf16[80,128]{1,0:T(8,128)(2,1)S(1)}, bf16[80,128]{1,0:T(8,128)(2,1)S(1)}, u32[]{:S(2)}, u32[]{:S(2)}) collective-permute-start(bf16[80,128]{1,0:T(8,128)(2,1)S(1)} %get-tuple-element.31), channel_id=1, source_target_pairs={{0,128},{128,0},{1,129},{129,1},{2,130},{130,2},{3,131},{131,3},{4... | collective-permute-start | bytes 61448 | tf_op jit(solution)/shard_map/ppermute | solution.py:546
  145.5 2.1 %order_posterior.1 = bf16[1,256,512]{2,1,0:T(8,128)(2,1)} custom-call(bf16[256,256]{1,0:T(8,128)(2,1)} %get-tuple-element.15.left_ref, bf16[256,256]{1,0:T(8,128)(2,1)} %get-tuple-element.16.right_ref.post_ref), custom_call_target="tpu_custom_call" | custom-call | tf_op jit(solution)/shard_map/order_posterior/pallas_call | solution.py:313
  (84 shorter events, 27.8 us)
Async XLA Ops:
  2.2 3.8 %collective-permute-start = (bf16[1,80,128]{2,1,0:T(8,128)(2,1)}, bf16[1,80,128]{2,1,0:T(8,128)(2,1)S(1)}, u32[]{:S(2)}, u32[]{:S(2)}) collective-permute-start(bf16[1,80,128]{2,1,0:T(8,128)(2,1)} %pack_sections.1), channel_id=1, source_target_pairs={{0,4},{1,5},{2,6},{3,7},{4,0},{5,1},{6,2},{7,3},{8,12},{9,13},{10,... | collective-permute-start | bytes 61448 | tf_op jit(solution)/shard_map/ppermute | solution.py:57
  6.7 6.8 %collective-permute-start.1 = (bf16[2,80,128]{2,1,0:T(8,128)(2,1)S(1)}, bf16[2,80,128]{2,1,0:T(8,128)(2,1)S(1)}, u32[]{:S(2)}, u32[]{:S(2)}) collective-permute-start(bf16[2,80,128]{2,1,0:T(8,128)(2,1)S(1)} %pad_maximum_fusion.7), channel_id=1, source_target_pairs={{0,28},{1,29},{2,30},{3,31},{4,8},{5,9},{6,10},{7,11},{8,4},{9,5},... | collective-permute-start | bytes 122888 | tf_op jit(solution)/shard_map/ppermute | solution.py:57
  14.3 6.0 %collective-permute-start.2 = (bf16[4,80,128]{2,1,0:T(8,128)(2,1)S(1)}, bf16[4,80,128]{2,1,0:T(8,128)(2,1)S(1)}, u32[]{:S(2)}, u32[]{:S(2)}) collective-permute-start(bf16[4,80,128]{2,1,0:T(8,128)(2,1)S(1)} %pad_maximum_fusion.6), channel_id=1, source_target_pairs={{0,12},{1,13},{2,14},{3,15},{4,24},{5,25},{6,26},{7,27},{8,20},{9,... | collective-permute-start | bytes 245768 | tf_op jit(solution)/shard_map/ppermute | solution.py:57
  22.5 4.9 %collective-permute-start.8 = (bf16[1,8,40,128]{3,2,1,0:T(8,128)(2,1)S(1)}, bf16[1,8,40,128]{3,2,1,0:T(8,128)(2,1)S(1)}, u32[]{:S(2)}, u32[]{:S(2)}) collective-permute-start(bf16[1,8,40,128]{3,2,1,0:T(8,128)(2,1)S(1)} %get-tuple-element.27), channel_id=1, source_target_pairs={{0,1},{1,0},{2,3},{3,2},{4,5},{5,4},{6,7},{7,6},{8,9},{9,8},{10,11... | collective-permute-start | bytes 245768 | tf_op jit(solution)/shard_map/ppermute | solution.py:49
  24.5 5.5 %collective-permute-start.4 = (bf16[2,8,40,128]{3,2,1,0:T(8,128)(2,1)S(1)}, bf16[2,8,40,128]{3,2,1,0:T(8,128)(2,1)S(1)}, u32[]{:S(2)}, u32[]{:S(2)}) collective-permute-start(bf16[2,8,40,128]{3,2,1,0:T(8,128)(2,1)S(1)} %pad_maximum_fusion.3), channel_id=1, source_target_pairs={{0,96},{1,97},{2,98},{3,99},{4,100},{5,101},{6,102},{7,103},{8,104... | collective-permute-start | bytes 491528 | tf_op jit(solution)/shard_map/ppermute | solution.py:49
  27.4 7.1 %collective-permute-start.9 = (bf16[2,8,40,128]{3,2,1,0:T(8,128)(2,1)S(1)}, bf16[2,8,40,128]{3,2,1,0:T(8,128)(2,1)S(1)}, u32[]{:S(2)}, u32[]{:S(2)}) collective-permute-start(bf16[2,8,40,128]{3,2,1,0:T(8,128)(2,1)S(1)} %pad_maximum_fusion.4), channel_id=1, source_target_pairs={{0,3},{1,2},{2,1},{3,0},{4,7},{5,6},{6,5},{7,4},{8,11},{9,10},{10,... | collective-permute-start | bytes 491528 | tf_op jit(solution)/shard_map/ppermute | solution.py:49
  30.1 7.6 %collective-permute-start.7 = (bf16[4,8,40,128]{3,2,1,0:T(8,128)(2,1)S(1)}, bf16[4,8,40,128]{3,2,1,0:T(8,128)(2,1)S(1)}, u32[]{:S(2)}, u32[]{:S(2)}) collective-permute-start(bf16[4,8,40,128]{3,2,1,0:T(8,128)(2,1)S(1)} %pad_maximum_fusion.a0), channel_id=1, source_target_pairs={{0,2},{1,3},{2,0},{3,1},{4,6},{5,7},{6,4},{7,5},{8,10},{9,11},{10,... | collective-permute-start | bytes 983048 | tf_op jit(solution)/shard_map/ppermute | solution.py:49
  33.6 20.6 %collective-permute-start.6 = (bf16[4,8,40,128]{3,2,1,0:T(8,128)(2,1)S(1)}, bf16[4,8,40,128]{3,2,1,0:T(8,128)(2,1)S(1)}, u32[]{:S(2)}, u32[]{:S(2)}) collective-permute-start(bf16[4,8,40,128]{3,2,1,0:T(8,128)(2,1)S(1)} %pad_maximum_fusion.a0), channel_id=1, source_target_pairs={{0,3},{1,2},{2,1},{3,0},{4,7},{5,6},{6,5},{7,4},{8,11},{9,10},{10,... | collective-permute-start | bytes 983048 | tf_op jit(solution)/shard_map/ppermute | solution.py:49
  34.5 19.7 %collective-permute-start.5 = (bf16[4,8,40,128]{3,2,1,0:T(8,128)(2,1)S(1)}, bf16[4,8,40,128]{3,2,1,0:T(8,128)(2,1)S(1)}, u32[]{:S(2)}, u32[]{:S(2)}) collective-permute-start(bf16[4,8,40,128]{3,2,1,0:T(8,128)(2,1)S(1)} %pad_maximum_fusion.a0), channel_id=1, source_target_pairs={{0,1},{1,0},{2,3},{3,2},{4,5},{5,4},{6,7},{7,6},{8,9},{9,8},{10,11... | collective-permute-start | bytes 983048 | tf_op jit(solution)/shard_map/ppermute | solution.py:49
  34.6 19.6 %collective-permute-start.12 = (bf16[4,8,40,128]{3,2,1,0:T(8,128)(2,1)S(1)}, bf16[4,8,40,128]{3,2,1,0:T(8,128)(2,1)S(1)}, u32[]{:S(2)}, u32[]{:S(2)}) collective-permute-start(bf16[4,8,40,128]{3,2,1,0:T(8,128)(2,1)S(1)} %pad_maximum_fusion.1.b0), channel_id=1, source_target_pairs={{0,32},{1,33},{2,34},{3,35},{4,36},{5,37},{6,38},{7,39},{8,40},{9,... | collective-permute-start | bytes 983048 | tf_op jit(solution)/shard_map/ppermute | solution.py:49
  36.4 17.8 %collective-permute-start.11 = (bf16[4,8,40,128]{3,2,1,0:T(8,128)(2,1)S(1)}, bf16[4,8,40,128]{3,2,1,0:T(8,128)(2,1)S(1)}, u32[]{:S(2)}, u32[]{:S(2)}) collective-permute-start(bf16[4,8,40,128]{3,2,1,0:T(8,128)(2,1)S(1)} %pad_maximum_fusion.1.b0), channel_id=1, source_target_pairs={{0,96},{1,97},{2,98},{3,99},{4,100},{5,101},{6,102},{7,103},{8,104... | collective-permute-start | bytes 983048 | tf_op jit(solution)/shard_map/ppermute | solution.py:49
  37.7 16.6 %collective-permute-start.10 = (bf16[4,8,40,128]{3,2,1,0:T(8,128)(2,1)S(1)}, bf16[4,8,40,128]{3,2,1,0:T(8,128)(2,1)S(1)}, u32[]{:S(2)}, u32[]{:S(2)}) collective-permute-start(bf16[4,8,40,128]{3,2,1,0:T(8,128)(2,1)S(1)} %pad_maximum_fusion.1.b0), channel_id=1, source_target_pairs={{0,64},{1,65},{2,66},{3,67},{4,68},{5,69},{6,70},{7,71},{8,72},{9,... | collective-permute-start | bytes 983048 | tf_op jit(solution)/shard_map/ppermute | solution.py:49
  79.5 16.9 %collective-permute-start.13 = (bf16[4,8,40,128]{3,2,1,0:T(8,128)(2,1)}, bf16[4,8,40,128]{3,2,1,0:T(8,128)(2,1)S(1)}, u32[]{:S(2)}, u32[]{:S(2)}) collective-permute-start(bf16[4,8,40,128]{3,2,1,0:T(8,128)(2,1)} %get-tuple-element.18), channel_id=1, source_target_pairs={{0,1},{1,0},{2,3},{3,2},{4,5},{5,4},{6,7},{7,6},{8,9},{9,8},{10,11... | collective-permute-start | bytes 983048 | tf_op jit(solution)/shard_map/ppermute | solution.py:49
  81.0 15.5 %collective-permute-start.14 = (bf16[4,8,40,128]{3,2,1,0:T(8,128)(2,1)}, bf16[4,8,40,128]{3,2,1,0:T(8,128)(2,1)S(1)}, u32[]{:S(2)}, u32[]{:S(2)}) collective-permute-start(bf16[4,8,40,128]{3,2,1,0:T(8,128)(2,1)} %get-tuple-element.19), channel_id=1, source_target_pairs={{0,3},{1,2},{2,1},{3,0},{4,7},{5,6},{6,5},{7,4},{8,11},{9,10},{10,... | collective-permute-start | bytes 983048 | tf_op jit(solution)/shard_map/ppermute | solution.py:49
  82.8 13.7 %collective-permute-start.15 = (bf16[4,8,40,128]{3,2,1,0:T(8,128)(2,1)}, bf16[4,8,40,128]{3,2,1,0:T(8,128)(2,1)S(1)}, u32[]{:S(2)}, u32[]{:S(2)}) collective-permute-start(bf16[4,8,40,128]{3,2,1,0:T(8,128)(2,1)} %get-tuple-element.20), channel_id=1, source_target_pairs={{0,2},{1,3},{2,0},{3,1},{4,6},{5,7},{6,4},{7,5},{8,10},{9,11},{10,... | collective-permute-start | bytes 983048 | tf_op jit(solution)/shard_map/ppermute | solution.py:49
  92.5 6.5 %collective-permute-start.18 = (bf16[4,8,40,128]{3,2,1,0:T(8,128)(2,1)}, bf16[4,8,40,128]{3,2,1,0:T(8,128)(2,1)S(1)}, u32[]{:S(2)}, u32[]{:S(2)}) collective-permute-start(bf16[4,8,40,128]{3,2,1,0:T(8,128)(2,1)} %get-tuple-element.22), channel_id=1, source_target_pairs={{0,64},{1,65},{2,66},{3,67},{4,68},{5,69},{6,70},{7,71},{8,72},{9,... | collective-permute-start | bytes 983048 | tf_op jit(solution)/shard_map/ppermute | solution.py:49
  93.7 10.9 %collective-permute-start.19 = (bf16[4,8,40,128]{3,2,1,0:T(8,128)(2,1)}, bf16[4,8,40,128]{3,2,1,0:T(8,128)(2,1)S(1)}, u32[]{:S(2)}, u32[]{:S(2)}) collective-permute-start(bf16[4,8,40,128]{3,2,1,0:T(8,128)(2,1)} %get-tuple-element.23), channel_id=1, source_target_pairs={{0,96},{1,97},{2,98},{3,99},{4,100},{5,101},{6,102},{7,103},{8,104... | collective-permute-start | bytes 983048 | tf_op jit(solution)/shard_map/ppermute | solution.py:49
  96.4 8.2 %collective-permute-start.20 = (bf16[4,8,40,128]{3,2,1,0:T(8,128)(2,1)}, bf16[4,8,40,128]{3,2,1,0:T(8,128)(2,1)S(1)}, u32[]{:S(2)}, u32[]{:S(2)}) collective-permute-start(bf16[4,8,40,128]{3,2,1,0:T(8,128)(2,1)} %get-tuple-element.24), channel_id=1, source_target_pairs={{0,32},{1,33},{2,34},{3,35},{4,36},{5,37},{6,38},{7,39},{8,40},{9,... | collective-permute-start | bytes 983048 | tf_op jit(solution)/shard_map/ppermute | solution.py:49
  96.8 11.2 %collective-permute-start.16 = (bf16[2,8,40,128]{3,2,1,0:T(8,128)(2,1)S(1)}, bf16[2,8,40,128]{3,2,1,0:T(8,128)(2,1)S(1)}, u32[]{:S(2)}, u32[]{:S(2)}) collective-permute-start(bf16[2,8,40,128]{3,2,1,0:T(8,128)(2,1)S(1)} %slice.67), channel_id=1, source_target_pairs={{0,96},{1,97},{2,98},{3,99},{4,100},{5,101},{6,102},{7,103},{8,104... | collective-permute-start | bytes 491528 | tf_op jit(solution)/shard_map/ppermute | solution.py:49
  105.8 5.8 %collective-permute-start.21 = (bf16[2,8,40,128]{3,2,1,0:T(8,128)(2,1)S(1)}, bf16[2,8,40,128]{3,2,1,0:T(8,128)(2,1)S(1)}, u32[]{:S(2)}, u32[]{:S(2)}) collective-permute-start(bf16[2,8,40,128]{3,2,1,0:T(8,128)(2,1)S(1)} %slice.71), channel_id=1, source_target_pairs={{0,3},{1,2},{2,1},{3,0},{4,7},{5,6},{6,5},{7,4},{8,11},{9,10},{10,... | collective-permute-start | bytes 491528 | tf_op jit(solution)/shard_map/ppermute | solution.py:49
  108.0 4.5 %collective-permute-start.17 = (bf16[1,8,40,128]{3,2,1,0:T(8,128)(2,1)S(1)}, bf16[1,8,40,128]{3,2,1,0:T(8,128)(2,1)S(1)}, u32[]{:S(2)}, u32[]{:S(2)}) collective-permute-start(bf16[1,8,40,128]{3,2,1,0:T(8,128)(2,1)S(1)} %slice.69), channel_id=1, source_target_pairs={{0,64},{1,65},{2,66},{3,67},{4,68},{5,69},{6,70},{7,71},{8,72},{9,... | collective-permute-start | bytes 245768 | tf_op jit(solution)/shard_map/ppermute | solution.py:49
  115.3 6.1 %collective-permute-start.23 = (bf16[4,80,128]{2,1,0:T(8,128)(2,1)S(1)}, bf16[4,80,128]{2,1,0:T(8,128)(2,1)S(1)}, u32[]{:S(2)}, u32[]{:S(2)}) collective-permute-start(bf16[4,80,128]{2,1,0:T(8,128)(2,1)S(1)} %pad_maximum_fusion.5), channel_id=1, source_target_pairs={{0,12},{1,13},{2,14},{3,15},{4,24},{5,25},{6,26},{7,27},{8,20},{9,... | collective-permute-start | bytes 245768 | tf_op jit(solution)/shard_map/ppermute | solution.py:57
  121.4 4.2 %collective-permute-start.24 = (bf16[2,80,128]{2,1,0:T(8,128)(2,1)S(1)}, bf16[2,80,128]{2,1,0:T(8,128)(2,1)S(1)}, u32[]{:S(2)}, u32[]{:S(2)}) collective-permute-start(bf16[2,80,128]{2,1,0:T(8,128)(2,1)S(1)} %slice.77), channel_id=1, source_target_pairs={{0,28},{1,29},{2,30},{3,31},{4,8},{5,9},{6,10},{7,11},{8,4},{9,5},... | collective-permute-start | bytes 122888 | tf_op jit(solution)/shard_map/ppermute | solution.py:57
  128.9 18.6 %collective-permute-start.26 = (bf16[80,128]{1,0:T(8,128)(2,1)S(1)}, bf16[80,128]{1,0:T(8,128)(2,1)S(1)}, u32[]{:S(2)}, u32[]{:S(2)}) collective-permute-start(bf16[80,128]{1,0:T(8,128)(2,1)S(1)} %get-tuple-element.31), channel_id=1, source_target_pairs={{0,128},{128,0},{1,129},{129,1},{2,130},{130,2},{3,131},{131,3},{4... | collective-permute-start | bytes 61448 | tf_op jit(solution)/shard_map/ppermute | solution.py:546
  (13 other events, 90.3 us)
